TPU v7x, 128 devices: a whole 4x4x4 slice. The times are simulated.
128 devices in a mesh: group: 8 (over x_lo, z), blk: 16 (over y, x_hi, core).
Axes of the slice: x: 4 (x_hi: 2, x_lo: 2; x = x_hi * 2 + x_lo), y: 4, z: 4, core: 2. Of those that a mesh axis runs over, the one named last changes fastest.
Arguments:
- cotangent: bfloat16 [98304, 3584], P(('group', 'blk')), may hold values from -24 to 24
- pre_act: bfloat16 [98304, 2, 1024], P(('group', 'blk')), may hold values from -6 to 6
- down_weight: bfloat16 [1024, 2, 3584], P('blk'), may hold values from -0.09375 to 0.09375
- tile_expert: int32 [768], P(('group', 'blk')), may hold values from 0 to 1
- tile_fill: int32 [768], P(('group', 'blk')), may hold values from 1 to 128, as said below
Outputs:
- act_grad: bfloat16 [98304, 2, 1024], P(('group', 'blk'))
- weight_grad: float32 [1024, 2, 3584], P(('group', 'blk'))
Inputs may be any that keep to these rules, and one draw needn't show every extreme that they name: tile_fill reaches 128 in every draw.
All inputs are finite; a program needn't handle non-finite values.
Results may differ from a plain program's by a relative error of at most 0.0029.
Values may be sent and summed in bfloat16 or wider, within the bound.
A program may use at most 192 MiB of HBM per device.

v0:
```python
import jax
import jax.numpy as jnp
from jax import lax
from jax.sharding import PartitionSpec as P

grad_factor = 0.015625


def body(cotangent, pre_act, down_weight, tile_expert, tile_fill):
    row_count = cotangent.shape[0]
    tile_count = tile_expert.shape[0]
    tile_size = row_count // tile_count
    width = cotangent.shape[1]
    hidden_units = pre_act.shape[2]
    expert_count = down_weight.shape[1]
    cot_tiles = cotangent.reshape(tile_count, tile_size, width)
    piece = lax.all_gather(down_weight, "blk", axis=0, tiled=True)
    chosen = jnp.take(piece, tile_expert, axis=1)
    result = jnp.einsum("trd,ntd->trn", cot_tiles, chosen, preferred_element_type=jnp.float32)
    hidden_grad = result.reshape(row_count, piece.shape[0])
    positions = jnp.arange(tile_size, dtype=jnp.int32)
    live_rows = (positions[None, :] < tile_fill[:, None]).astype(jnp.float32).reshape(row_count, 1)
    gate_pre = pre_act[:, 0, :].astype(jnp.float32)
    up_pre = pre_act[:, 1, :].astype(jnp.float32)
    sigmoid_gate = jax.nn.sigmoid(gate_pre)
    silu_gate = gate_pre * sigmoid_gate
    activation = (live_rows * silu_gate * up_pre).astype(jnp.bfloat16)
    gate_grad = (
        live_rows * hidden_grad * up_pre * sigmoid_gate * (1.0 + gate_pre * (1.0 - sigmoid_gate))
    )
    up_grad = live_rows * hidden_grad * silu_gate
    act_grad = jnp.stack([gate_grad, up_grad], axis=1).astype(jnp.bfloat16)
    expert_hot = tile_expert[:, None] == jnp.arange(expert_count, dtype=jnp.int32)[None, :]
    group_count = lax.axis_size("group")
    blk_count = lax.axis_size("blk")
    block_rows = hidden_units // (group_count * blk_count)
    reordered = activation.reshape(row_count, group_count, blk_count, block_rows)
    reordered = jnp.swapaxes(reordered, 1, 2).reshape(tile_count, tile_size, 1, hidden_units)
    act_expert = jnp.where(expert_hot[:, None, :, None], reordered, jnp.zeros((), jnp.bfloat16))
    partial_value = lax.psum_scatter(
        jnp.einsum("treh,trd->hed", act_expert, cot_tiles, preferred_element_type=jnp.float32),
        "blk",
        scatter_dimension=0,
        tiled=True,
    )
    total = lax.psum_scatter(partial_value, "group", scatter_dimension=0, tiled=True)
    return (act_grad, total * grad_factor)


def solution(mesh):
    placed = (
        P(("group", "blk"), None),
        P(("group", "blk"), None, None),
        P("blk", None, None),
        P(("group", "blk")),
        P(("group", "blk")),
    )
    return jax.shard_map(
        body,
        mesh=mesh,
        in_specs=placed,
        out_specs=(P(("group", "blk"), None, None), P(("group", "blk"), None, None)),
        check_vma=False,
    )
```

profile of v0, /device:TPU:0, one launch (start us, length us, event | category | flops | bytes accessed | tf_op | source)
XLA Modules:
  0.0 378.6 jit_solution(13612688103690177794)
XLA Ops:
  7.2 0.7 all-gather.2.cloned.1.call-update
  7.9 0.0 reduce-scatter.3.cloned.1.call-start
  7.9 9.4 %fusion.18 = (bf16[768,1,1024]{2,1,0:T(2,128)(2,1)}, bf16[768,1,1024]{2,1,0:T(2,128)(2,1)}) fusion(bf16[768,2,1024]{2,1,0:T(2,128)(2,1)} %param.6), kind=kLoop, calls=%fused_computation.36 | loop fusion | bytes 6291456 | tf_op jit(solution)/shard_map/slice | solution.py:24
  17.4 6.8 %copy.37 = bf16[768,1,1024]{0,2,1:T(8,128)(2,1)S(1)} copy(bf16[768,1,1024]{2,1,0:T(2,128)(2,1)} %get-tuple-element.14) | data formatting | bytes 3145728
  24.2 7.1 %copy.38 = bf16[768,1,1024]{0,2,1:T(8,128)(2,1)S(1)} copy(bf16[768,1,1024]{2,1,0:T(2,128)(2,1)} %get-tuple-element.15) | data formatting | bytes 3145728
  31.3 0.1 convert_bitcast_fusion
  31.4 0.7 copy-done.4
  32.1 1.1 fusion.13
  33.2 1.3 copy.27
  34.6 4.3 %broadcast_in_dim.43 = bf16[6,128,1024]{1,0,2:T(8,128)(2,1)} reshape(bf16[768,16,8,8]{0,3,2,1:T(8,128)(2,1)} %copy.27) | data formatting | bytes 3145728 | tf_op jit(solution)/shard_map/jit(_where)/broadcast_in_dim | solution.py:39
  38.9 1.8 copy.28
  40.7 18.5 %convolution_bitcast_fusion = f32[1024,2,3584]{2,0,1:T(8,128)} fusion(bf16[6,128,3584,1]{2,1,0,3:T(8,128)(2,1)} %bitcast.36, pred[6,2]{0,1:T(4,128)(4,1)S(1)} %iota_compare_fusion.1, bf16[6,128,1024]{1,2,0:T(8,128)(2,1)S(1)} %copy.28), kind=kOutput, calls=%fused_computation.14 | convolution fusion | flops 11275862016 | bytes 36438028 | tf_op jit(solution)/shard_map/treh,trd->hed/dot_general | solution.py:41
  59.3 0.2 reduce-scatter.5.cloned.1.call-start
  59.5 53.0 %all-gather.2.cloned.1.call-done = bf16[1024,2,3584]{2,1,0:T(2,128)(2,1)} async-done(((bf16[64,2,3584]{2,1,0:T(2,128)(2,1)}), bf16[1024,2,3584]{2,1,0:T(2,128)(2,1)}) %all-gather.2.cloned.1.call-update) | async-done | bytes 14680080 | tf_op jit(solution)/shard_map/all_gather | solution.py:17
  112.5 15.7 %fusion.17 = (bf16[1024,2,896]{2,1,0:T(2,128)(2,1)}, bf16[1024,2,896]{2,1,0:T(2,128)(2,1)}, bf16[1024,2,896]{2,1,0:T(2,128)(2,1)}, bf16[1024,2,896]{2,1,0:T(2,128)(2,1)}) fusion(bf16[1024,2,3584]{2,1,0:T(2,128)(2,1)} %all-gather.2.cloned.1.call-done), kind=kLoop, calls=%fused_computation.35 | loop fusion | bytes 29360128 | tf_op jit(solution)/shard_map/jit(_take)/gather | solution.py:18
  128.2 10.4 %copy.33 = bf16[1024,2,896]{0,2,1:T(8,128)(2,1)} copy(bf16[1024,2,896]{2,1,0:T(2,128)(2,1)} %get-tuple-element.8) | data formatting | bytes 7340032
  138.6 10.4 %copy.34 = bf16[1024,2,896]{0,2,1:T(8,128)(2,1)} copy(bf16[1024,2,896]{2,1,0:T(2,128)(2,1)} %get-tuple-element.10) | data formatting | bytes 7340032
  149.0 9.2 %gather_fusion = bf16[6,1024,896]{1,2,0:T(8,128)(2,1)} fusion(bf16[1024,2,896]{0,2,1:T(8,128)(2,1)} %copy.33, s32[1024]{0:T(1024)S(1)} %pad_clamp_fusion), kind=kCustom, calls=%fused_computation | custom fusion | bytes 22020120 | tf_op jit(solution)/shard_map/jit(_take)/gather | solution.py:18
  158.2 8.2 %gather_fusion.1 = bf16[6,1024,896]{1,2,0:T(8,128)(2,1)} fusion(bf16[1024,2,896]{0,2,1:T(8,128)(2,1)} %copy.34, s32[1024]{0:T(1024)S(1)} %pad_clamp_fusion), kind=kCustom, calls=%fused_computation.1 | custom fusion | bytes 22020120 | tf_op jit(solution)/shard_map/jit(_take)/gather | solution.py:18
  166.4 10.0 %copy.35 = bf16[1024,2,896]{0,2,1:T(8,128)(2,1)} copy(bf16[1024,2,896]{2,1,0:T(2,128)(2,1)} %get-tuple-element.9) | data formatting | bytes 7340032
  176.5 8.3 %gather_fusion.2 = bf16[6,1024,896]{1,2,0:T(8,128)(2,1)} fusion(bf16[1024,2,896]{0,2,1:T(8,128)(2,1)} %copy.35, s32[1024]{0:T(1024)S(1)} %pad_clamp_fusion), kind=kCustom, calls=%fused_computation.2 | custom fusion | bytes 22020120 | tf_op jit(solution)/shard_map/jit(_take)/gather | solution.py:18
  184.7 9.9 %copy.36 = bf16[1024,2,896]{0,2,1:T(8,128)(2,1)} copy(bf16[1024,2,896]{2,1,0:T(2,128)(2,1)} %get-tuple-element.11) | data formatting | bytes 7340032
  194.7 8.5 %gather_fusion.3 = bf16[6,1024,896]{1,2,0:T(8,128)(2,1)} fusion(bf16[1024,2,896]{0,2,1:T(8,128)(2,1)} %copy.36, s32[1024]{0:T(1024)S(1)} %pad_clamp_fusion), kind=kCustom, calls=%fused_computation.3 | custom fusion | bytes 22020120 | tf_op jit(solution)/shard_map/jit(_take)/gather | solution.py:18
  203.1 124.7 %reduce-scatter.3.cloned.1.call-done = f32[64,2,3584]{2,0,1:T(8,128)} async-done(((f32[1024,2,3584]{2,0,1:T(8,128)}), f32[64,2,3584]{2,0,1:T(8,128)}) %reduce-scatter.3.cloned.1.call-update) | async-done | bytes 1835024 | tf_op jit(solution)/shard_map/reduce_scatter | solution.py:40
  327.9 19.7 %fusion = f32[6,1024,128]{1,2,0:T(8,128)} fusion(bf16[6,128,3584]{2,1,0:T(8,128)(2,1)} %bitcast.37, bf16[1024,6,896]{0,2,1:T(8,128)(2,1)} %bitcast.32, bf16[1024,6,896]{0,2,1:T(8,128)(2,1)} %bitcast.31, bf16[1024,6,896]{0,2,1:T(8,128)(2,1)} %bitcast.30, bf16[1024,6,896]{0,2,1:T(8,128)(2,1)} %bitcast.29, pred[6]{0:T(512)(128)(4,1)S(1)} %compare_and_fusion), kind=kOutput, calls=%fused_computation.5 | convolution fusion | flops 5835325440 | bytes 52690952 | tf_op jit(solution)/shard_map/trd,ntd->trn/dot_general | solution.py:19
  347.6 3.7 copy.24
  351.3 3.5 multiply_convert_fusion.2
  354.9 0.3 pad_maximum_fusion
  355.2 5.8 %copy.29 = bf16[768,2,1024]{2,1,0:T(2,128)(2,1)} copy(bf16[768,2,1024]{0,2,1:T(8,128)(2,1)S(1)} %pad_maximum_fusion) | data formatting | bytes 6291456
  360.9 9.3 %reduce-scatter.5.cloned.1.call-done = f32[8,2,3584]{2,0,1:T(8,128)} async-done(((f32[64,2,3584]{2,0,1:T(8,128)}), f32[8,2,3584]{2,0,1:T(8,128)}) %reduce-scatter.5.cloned.1.call-update) | async-done | bytes 229392 | tf_op jit(solution)/shard_map/reduce_scatter | solution.py:46
  370.3 1.0 broadcast_multiply_fusion
  371.2 0.9 copy.30
  (22 shorter events, 0.1 us)
Async XLA Ops:
  7.2 105.4 %all-gather.2.cloned.1.call-start = ((), (), s32[]{:S(2)}) async-start(), calls=%async_computation.2 | async-start | bytes 15597568 | tf_op jit(solution)/shard_map/all_gather | solution.py:17
  7.9 320.0 %reduce-scatter.3.cloned.1.call-start = ((), (), s32[]{:S(2)}) async-start(), calls=%async_computation.3 | async-start | bytes 31195136 | tf_op jit(solution)/shard_map/reduce_scatter | solution.py:40
  24.1 9.1 %copy-start = (bf16[768,1,1024]{0,2,1:T(8,128)(2,1)}, bf16[768,1,1024]{0,2,1:T(8,128)(2,1)S(1)}, u32[]{:S(2)}) copy-start(bf16[768,1,1024]{0,2,1:T(8,128)(2,1)S(1)} %copy.37) | copy-start | bytes 4718596
  24.2 7.2 %copy-start.6 = (s32[6]{0:T(128)S(1)}, s32[6]{0:T(128)}, u32[]{:S(2)}) copy-start(s32[6]{0:T(128)} %param.9) | copy-start | bytes 76
  31.3 3.2 copy-start.2
  31.4 0.7 copy-start.4
  34.6 6.1 %copy-start.7 = (s32[6]{0:T(128)S(1)}, s32[6]{0:T(128)}, u32[]{:S(2)}) copy-start(s32[6]{0:T(128)} %param.8) | copy-start | bytes 76
  59.3 311.0 %reduce-scatter.5.cloned.1.call-start = ((), (), s32[]{:S(2)}) async-start(), calls=%async_computation.4 | async-start | bytes 2064384 | tf_op jit(solution)/shard_map/reduce_scatter | solution.py:46
  347.6 3.7 copy-start.1
  347.6 3.7 copy-start.3
  347.6 3.7 copy-start.5
Sparse Core Ops, SparseCore 0:
  10.5 102.0 all-gather.1
  116.9 210.9 reduce-scatter.2
  330.3 39.9 reduce-scatter.4
where the time goes:
time: 381 us; the launch traced here: 379 us
  waiting for transfers between devices  188 us (49%)
  local copies, waits for them, and re-layouts  132 us (35%)
  matrix products  38.3 us (10%)
  between operations  13.9 us (4%)
  other arithmetic  5.99 us (2%)
    reduce_scatter x1, waiting for transfers between devices, body(): lax.psum_scatter(jnp.einsum('treh,trd->hed', act_expert, cot_tiles, prefe...  125 us
    unnamed x24, local copies, waits for them, and re-layouts  62 us
    all_gather x1, waiting for transfers between devices, body(): piece = lax.all_gather(down_weight, 'blk', axis=0, tiled=True)  53 us
    gather x5, local copies, waits for them, and re-layouts, body(): chosen = jnp.take(piece, tile_expert, axis=1)  49.8 us
    dot_general x1, matrix products, body(): jnp.einsum('trd,ntd->trn', cot_tiles, chosen, preferred_element_type=jnp....  19.7 us
    dot_general x1, matrix products, body(): jnp.einsum('treh,trd->hed', act_expert, cot_tiles, preferred_element_type...  18.5 us
    slice x1, local copies, waits for them, and re-layouts, body(): up_pre = pre_act[:, 1, :].astype(jnp.float32)  9.44 us
    reduce_scatter x1, waiting for transfers between devices, body(): lax.psum_scatter(partial_value, 'group', scatter_dimension=0, tiled=True)  9.35 us
  transfers between devices with their start and end apart: 3, of which 3 were waited for; matrix products, arithmetic and copies ran while one was open for 46% of the time, Pallas kernels for 0%

commit v1 on v0

v1 whole, which is shorter than its diff:
```python
import functools

import jax
import jax.numpy as jnp
from jax import lax
from jax.experimental import pallas as pl
from jax.experimental.pallas import tpu as pltpu
from jax.sharding import PartitionSpec as P

MESH = pl.DeviceIdType.MESH
grad_factor = 0.015625

ROWS = 768
WIDTH = 3584
WIDE = 512
CHUNKS = WIDTH // WIDE
COLS = 256
STAGE_ROWS = (256, 64, 16)
STAGE_TYPES = (jnp.bfloat16, jnp.bfloat16, jnp.float32)
f32 = jnp.float32


def kernel(
    cot_hbm, lhs_hbm, w_hbm, hot_ref,
    hidden_hbm, wgrad_hbm,
    cot_own, cot_sib, lhs, w_all, hg_buf, out_buf,
    own0, own1, own2, rel0, rel1, rel2, tot0, tot1,
    far0, far1, far2, up0, up1, up2, dn0, dn1, dn2,
    rfar0, rfar1, rfar2, rup0, rup1, rup2, rdn0, rdn1, rdn2,
    cot_sem, lhs_sem, w_sem, hg_sem, out_sem,
    cs_send, cs_recv, ls_send, ls_recv,
    ag_send, ag_recv, sib_send, sib_recv,
    s0_send, s0_recv, s1_send, s1_recv, s2_send, s2_recv,
):
    g = lax.axis_index("group")
    b = lax.axis_index("blk")
    x_lo, z = lax.div(g, 4), lax.rem(g, 4)
    y, c = lax.div(b, 4), lax.rem(b, 2)
    x_hi = lax.rem(lax.div(b, 2), 2)
    x = x_hi * 2 + x_lo

    def device(dx, dy, dz, core):
        xx, yy, zz = lax.rem(x + dx, 4), lax.rem(y + dy, 4), lax.rem(z + dz, 4)
        return (lax.rem(xx, 2) * 4 + zz, yy * 4 + lax.div(xx, 2) * 2 + core)

    other = 1 - c
    sibling = device(0, 0, 0, other)
    x_up, x_dn = device(1, 0, 0, c), device(3, 0, 0, c)
    y_up, y_dn = device(0, 1, 0, c), device(0, 3, 0, c)
    z_up, z_dn = device(0, 0, 1, c), device(0, 0, 3, c)
    x_peer = device(3 - 2 * x + 4, 0, 0, c)

    barrier = pltpu.get_barrier_semaphore()
    for peer in (sibling, x_up, x_dn, y_up, y_dn, z_up, z_dn):
        pl.semaphore_signal(barrier, inc=1, device_id=peer, device_id_type=MESH)

    def cot_cols(k):
        return pl.ds(pl.multiple_of(k * WIDE, WIDE), WIDE)

    def cot_copy(k):
        return pltpu.make_async_copy(cot_hbm.at[:, cot_cols(k)], cot_own.at[:, cot_cols(k)], cot_sem.at[k])

    def lhs_copy():
        return pltpu.make_async_copy(lhs_hbm.at[c], lhs.at[0], lhs_sem)

    q_own = y * 2 + x_hi

    def w_copy(e):
        return pltpu.make_async_copy(w_hbm.at[e], w_all.at[q_own, e, c], w_sem.at[e])

    for e in range(2):
        w_copy(e).start()
    lhs_copy().start()

    @pl.loop(0, CHUNKS)
    def _(k):
        cot_copy(k).start()

    pl.semaphore_wait(barrier, 7)

    def remote(src, dst, send, recv, device_id):
        return pltpu.make_async_remote_copy(
            src_ref=src, dst_ref=dst, send_sem=send, recv_sem=recv, device_id=device_id, device_id_type=MESH
        )

    def lhs_remote():
        return remote(lhs_hbm.at[other], lhs.at[1], ls_send, ls_recv, sibling)

    def cot_remote(k):
        return remote(
            cot_hbm.at[:, cot_cols(k)], cot_sib.at[:, cot_cols(k)], cs_send.at[k], cs_recv.at[k], sibling
        )

    def piece(j):
        yy = lax.rem(y + (0, 3, 1, 2)[j % 4], 4)
        return yy * 2 + (x_hi if j < 4 else 1 - x_hi)

    def gather(src_j, dst_j, e, slot, device_id):
        block = w_all.at[piece(src_j), e, c]
        return remote(block, block, ag_send.at[slot], ag_recv.at[dst_j, e], device_id)

    def gather_wait(j, e):
        block = w_all.at[piece(j), e, c]
        remote(block, block, ag_send.at[0], ag_recv.at[j, e], sibling).wait_recv()

    def share(j, e):
        block = w_all.at[piece(j), e, c]
        return remote(block, block, sib_send.at[j, e], sib_recv.at[j, e], sibling)

    def share_wait(j, e):
        block = w_all.at[piece(j), e, other]
        remote(block, block, sib_send.at[j, e], sib_recv.at[j, e], sibling).wait_recv()

    sends = []
    for e in range(2):
        sends += [(0, 1, e, y_up), (0, 2, e, y_dn), (0, 4, e, x_peer)]
    sends += [(1, 3, 0, y_up), (2, 3, 1, y_dn)]
    for e in range(2):
        sends += [(4, 5, e, y_up), (4, 6, e, y_dn)]
    sends += [(5, 7, 0, y_up), (6, 7, 1, y_dn)]

    def gather_start(j):
        for slot, (src, dst, e, device_id) in enumerate(sends):
            if src == j:
                gather(src, dst, e, slot, device_id).start()

    def arrived(j):
        for e in range(2):
            gather_wait(j, e)
        gather_start(j)
        for e in range(2):
            share(j, e).start()

    lhs_remote().start()
    cot_remote(0).start()
    for e in range(2):
        w_copy(e).wait()
    gather_start(0)

    @pl.loop(1, CHUNKS)
    def _(k):
        cot_remote(k).start()

    for e in range(2):
        share(0, e).start()

    own, rel, tot = (own0, own1, own2), (rel0, rel1, rel2), (tot0, tot1)
    far, up, dn = (far0, far1, far2), (up0, up1, up2), (dn0, dn1, dn2)
    rfar, rup, rdn = (rfar0, rfar1, rfar2), (rup0, rup1, rup2), (rdn0, rdn1, rdn2)
    s_send, s_recv = (s0_send, s1_send, s2_send), (s0_recv, s1_recv, s2_recv)
    z_ring, x_ring, y_ring = (z, z_up, z_dn), (x, x_up, x_dn), (y, y_up, y_dn)
    rings = ((z_ring, x_ring, y_ring), (x_ring, z_ring, y_ring))

    def far_copy(s, st, n, half):
        rows = STAGE_ROWS[s] // 2
        _, plus, minus = rings[st][s]
        return remote(
            far[s].at[n, pl.ds(half * rows, rows)], rfar[s].at[n, pl.ds(half * rows, rows)],
            s_send[s].at[n, half], s_recv[s].at[n, half], (plus, minus)[half],
        )

    def near_copy(s, st, n, way):
        _, plus, minus = rings[st][s]
        return remote(
            (up, dn)[way][s].at[n], (rup, rdn)[way][s].at[n],
            s_send[s].at[n, 2 + way], s_recv[s].at[n, 2 + way], (plus, minus)[way],
        )

    def produce(s, st, n, block):
        half = STAGE_ROWS[s] // 2
        kind = STAGE_TYPES[s]
        far[s][n] = block(2).astype(kind)
        far_copy(s, st, n, 0).start()
        far_copy(s, st, n, 1).start()
        value = block(1)
        rel[s][lax.rem(n, 4), 0] = value[:half]
        up[s][n, half:] = value[half:].astype(kind)
        value = block(3)
        rel[s][lax.rem(n, 4), 1] = value[half:]
        dn[s][n, :half] = value[:half].astype(kind)
        own[s][n] = block(0)

    def relay(s, st, n):
        half = STAGE_ROWS[s] // 2
        kind = STAGE_TYPES[s]
        far_copy(s, st, n, 0).wait_recv()
        up[s][n, :half] = (rel[s][lax.rem(n, 4), 0] + rfar[s][n, :half].astype(f32)).astype(kind)
        near_copy(s, st, n, 0).start()
        far_copy(s, st, n, 1).wait_recv()
        dn[s][n, half:] = (rel[s][lax.rem(n, 4), 1] + rfar[s][n, half:].astype(f32)).astype(kind)
        near_copy(s, st, n, 1).start()

    def total(s, st, n):
        near_copy(s, st, n, 0).wait_recv()
        near_copy(s, st, n, 1).wait_recv()
        return own[s][n] + rup[s][n].astype(f32) + rdn[s][n].astype(f32)

    def first(st, k):
        cols = pl.ds(pl.multiple_of(k * WIDE + st * COLS, COLS), COLS)
        me = (z, x)[st]

        def block(offset):
            at = lax.rem(me + offset, 4)
            value = None
            for src, cot in ((0, cot_own), (1, cot_sib)):
                rows = lhs[src, at] if st == 0 else lhs[src, :, at]
                part = jnp.dot(rows.reshape(256, ROWS), cot[:, cols], preferred_element_type=f32)
                value = part if value is None else value + part
            return value

        produce(0, st, k * 2 + st, block)

    def onward(s, st, n):
        tot[s][st] = total(s, st, n)
        me = rings[st][s + 1][0]
        rows = STAGE_ROWS[s + 1]

        def block(offset):
            at = lax.rem(me + offset, 4) * rows
            return tot[s][st, pl.ds(pl.multiple_of(at, rows), rows), :]

        produce(s + 1, st, n, block)

    def last(st, n):
        cols = pl.ds(pl.multiple_of(n * COLS, COLS), COLS)
        out_buf[:, cols] = total(2, st, n) * grad_factor

    order = (0, 1, 2, 4, 3, 5, 6, 7)

    def hg_copy(turn):
        cols = pl.ds(pl.multiple_of(piece(order[turn]) * 128, 128), 128)
        return pltpu.make_async_copy(hg_buf.at[turn % 2], hidden_hbm.at[:, cols], hg_sem.at[turn])

    def hidden(turn):
        j = order[turn]
        for e in range(2):
            share_wait(j, e)
        if turn >= 2:
            hg_copy(turn - 2).wait()
        q = piece(j)

        @pl.loop(0, ROWS // 256)
        def _(m):
            rows = pl.ds(pl.multiple_of(m * 256, 256), 256)
            each = lax.dot_general(
                cot_own[rows, :], w_all[q].reshape(256, WIDTH), (((1,), (1,)), ((), ())), preferred_element_type=f32
            )
            hg_buf[turn % 2, rows, :] = jnp.where(hot_ref[rows, :] > 0.5, each[:, 128:], each[:, :128])

        hg_copy(turn).start()

    lhs_copy().wait()
    lhs_remote().wait_recv()

    events = {3: "12", 4: "4", 6: "3", 7: "56", 9: "7"}
    turns = {6: (0,), 7: (1,), 8: (2,), 9: (3, 4), 10: (5,), 11: (6,), 12: (7,)}

    @pl.loop(0, CHUNKS + 6)
    def _(t):
        def at(lag, do):
            @pl.when(jnp.logical_and(t >= lag, t < CHUNKS + lag))
            def _():
                do(t - lag)

        def make(k):
            cot_copy(k).wait()
            cot_remote(k).wait_recv()
            for st in range(2):
                first(st, k)

        def both(do):
            def run(k):
                for st in range(2):
                    do(st, k * 2 + st)

            return run

        at(0, make)
        at(1, both(lambda st, n: relay(0, st, n)))
        at(2, both(lambda st, n: onward(0, st, n)))
        at(3, both(lambda st, n: relay(1, st, n)))
        at(4, both(lambda st, n: onward(1, st, n)))
        at(5, both(lambda st, n: relay(2, st, n)))
        at(6, both(last))
        def on(when, do):
            @pl.when(t == when)
            def _():
                do()

        for when in range(CHUNKS + 6):
            for j in events.get(when, ""):
                on(when, functools.partial(arrived, int(j)))
            for turn in turns.get(when, ()):
                on(when, functools.partial(hidden, turn))

    out = pltpu.make_async_copy(out_buf, wgrad_hbm, out_sem)
    out.start()
    for turn in (6, 7):
        hg_copy(turn).wait()
    out.wait()

    lhs_remote().wait_send()

    @pl.loop(0, CHUNKS)
    def _(k):
        cot_remote(k).wait_send()
        for st in range(2):
            for s in range(3):
                for i in range(2):
                    far_copy(s, st, k * 2 + st, i).wait_send()
                    near_copy(s, st, k * 2 + st, i).wait_send()

    for slot, (src, dst, e, device_id) in enumerate(sends):
        gather(src, dst, e, slot, device_id).wait_send()
    for j in range(8):
        for e in range(2):
            share(j, e).wait_send()


def call(cot, lhs, w, hot):
    n = 2 * CHUNKS
    dma = pltpu.SemaphoreType.DMA
    any_space = pl.BlockSpec(memory_space=pl.ANY)

    def stages(shape, kind=None):
        return [pltpu.VMEM(shape(r), kind or t) for r, t in zip(STAGE_ROWS, STAGE_TYPES)]

    return pl.pallas_call(
        kernel,
        out_shape=(
            jax.ShapeDtypeStruct((ROWS, 1024), f32),
            jax.ShapeDtypeStruct((16, WIDTH), f32),
        ),
        in_specs=[any_space, any_space, any_space, pl.BlockSpec(memory_space=pltpu.VMEM)],
        out_specs=(any_space, any_space),
        scratch_shapes=[
            pltpu.VMEM((ROWS, WIDTH), jnp.bfloat16),
            pltpu.VMEM((ROWS, WIDTH), jnp.bfloat16),
            pltpu.VMEM((2, 4, 4, 64, ROWS), jnp.bfloat16),
            pltpu.VMEM((8, 2, 2, 64, WIDTH), jnp.bfloat16),
            pltpu.VMEM((2, ROWS, 128), f32),
            pltpu.VMEM((16, WIDTH), f32),
            *stages(lambda r: (n, r, COLS), f32),
            *stages(lambda r: (4, 2, r // 2, COLS), f32),
            *[pltpu.VMEM((2, r, COLS), f32) for r in STAGE_ROWS[:2]],
            *stages(lambda r: (n, r, COLS)),
            *stages(lambda r: (n, r, COLS)),
            *stages(lambda r: (n, r, COLS)),
            *stages(lambda r: (n, r, COLS)),
            *stages(lambda r: (n, r, COLS)),
            *stages(lambda r: (n, r, COLS)),
            dma((CHUNKS,)), dma, dma((2,)), dma((8,)), dma,
            dma((CHUNKS,)), dma((CHUNKS,)), dma, dma,
            dma((14,)), dma((8, 2)), dma((8, 2)), dma((8, 2)),
            dma((n, 4)), dma((n, 4)), dma((n, 4)), dma((n, 4)), dma((n, 4)), dma((n, 4)),
        ],
        compiler_params=pltpu.CompilerParams(
            collective_id=0, has_side_effects=True, vmem_limit_bytes=60 * 2**20
        ),
        cost_estimate=pl.CostEstimate(flops=24 * 10**9, bytes_accessed=30 * 10**6, transcendentals=0),
    )(cot, lhs, w, hot)


def body(cotangent, pre_act, down_weight, tile_expert, tile_fill):
    row_count = cotangent.shape[0]
    tile_count = tile_expert.shape[0]
    tile_size = row_count // tile_count
    expert_count = down_weight.shape[1]
    positions = jnp.arange(tile_size, dtype=jnp.int32)
    live_rows = (positions[None, :] < tile_fill[:, None]).astype(f32).reshape(row_count, 1)
    row_expert = jnp.repeat(tile_expert, tile_size)
    gate_pre = pre_act[:, 0, :].astype(f32)
    up_pre = pre_act[:, 1, :].astype(f32)
    sigmoid_gate = jax.nn.sigmoid(gate_pre)
    silu_gate = gate_pre * sigmoid_gate
    activation = (live_rows * silu_gate * up_pre).astype(jnp.bfloat16)
    parts = activation.reshape(row_count, 2, 4, 4, 2, 2, 8).transpose(5, 2, 4, 1, 3, 6, 0)
    expert_hot = row_expert[None, :] == jnp.arange(expert_count, dtype=jnp.int32)[:, None]
    lhs = jnp.where(expert_hot[:, None, :], parts[:, :, :, :, :, None], jnp.zeros((), jnp.bfloat16))
    lhs = lhs.reshape(2, 4, 4, 64, row_count)
    weights = jnp.swapaxes(down_weight, 0, 1)
    hot = jnp.broadcast_to((row_expert == 1).astype(f32)[:, None], (row_count, 128))
    hidden_grad, partial = call(cotangent, lhs, weights, hot)
    gate_grad = (
        live_rows * hidden_grad * up_pre * sigmoid_gate * (1.0 + gate_pre * (1.0 - sigmoid_gate))
    )
    up_grad = live_rows * hidden_grad * silu_gate
    act_grad = jnp.stack([gate_grad, up_grad], axis=1).astype(jnp.bfloat16)
    return act_grad, jnp.swapaxes(partial.reshape(2, 8, WIDTH), 0, 1)


def solution(mesh):
    placed = (
        P(("group", "blk"), None),
        P(("group", "blk"), None, None),
        P("blk", None, None),
        P(("group", "blk")),
        P(("group", "blk")),
    )
    return jax.shard_map(
        body,
        mesh=mesh,
        in_specs=placed,
        out_specs=(P(("group", "blk"), None, None), P(("group", "blk"), None, None)),
        check_vma=False,
    )
```

time: 381 us -> 144 us (0.38)
  waiting for transfers between devices: 188 us -> 0 us
  local copies, waits for them, and re-layouts: 132 us -> 23.9 us
  Pallas kernels: 0 us -> 104 us
  matrix products: 38.3 us -> 0 us
  between operations: 13.9 us -> 0.73 us
  other arithmetic: 5.99 us -> 15.4 us
    reduce_scatter x2 -> x0, waiting for transfers between devices: 134 us -> none  [the longest x1 125 us: body(): lax.psum_scatter(jnp.einsum('treh,trd->hed', act_expert, cot_tiles, prefe...]
    pallas_call x0 -> x1, Pallas kernels: none -> 104 us  [call(): pl.pallas_call(kernel, out_shape=(jax.ShapeDtypeStruct((ROWS, 1024), f32)...]
    unnamed x24 -> x12, local copies, waits for them, and re-layouts: 62 us -> 6.36 us
    all_gather x1 -> x0, waiting for transfers between devices: 53 us -> none  [body(): piece = lax.all_gather(down_weight, 'blk', axis=0, tiled=True)]
    gather x5 -> x0, local copies, waits for them, and re-layouts: 49.8 us -> none  [body(): chosen = jnp.take(piece, tile_expert, axis=1)]
    dot_general x2 -> x0, matrix products: 38.3 us -> none  [the longest x1 19.7 us: body(): jnp.einsum('trd,ntd->trn', cot_tiles, chosen, preferred_element_type=jnp....]
    convert_element_type x0 -> x2, local copies, waits for them, and re-layouts: none -> 7.19 us  [the longest x1 3.62 us: body(): up_pre = pre_act[:, 1, :].astype(f32)]
    broadcast_in_dim x2 -> x3, local copies, waits for them, and re-layouts: 6.12 us -> 1.17 us  [the longest x1 0.91 us: body(): jnp.broadcast_to((row_expert == 1).astype(f32)[:, None], (row_count, 128))]
  transfers between devices with their start and end apart: 3 -> 0, of which waited for: 3 -> 0; matrix products, arithmetic and copies ran while one was open for 46% -> 0% of each run, Pallas kernels for 0% -> 0%
where the time goes in v1:
time: 144 us
  Pallas kernels  104 us (72%)
  local copies, waits for them, and re-layouts  23.9 us (17%)
  other arithmetic  15.4 us (11%)
    pallas_call x1, Pallas kernels, call(): pl.pallas_call(kernel, out_shape=(jax.ShapeDtypeStruct((ROWS, 1024), f32)...  104 us
    slice x1, local copies, waits for them, and re-layouts, body(): gate_pre = pre_act[:, 0, :].astype(f32)  8 us
    unnamed x12, local copies, waits for them, and re-layouts  6.36 us
    another operation x2, other arithmetic, body(): act_grad = jnp.stack([gate_grad, up_grad], axis=1).astype(jnp.bfloat16)  5.16 us
    convert_element_type x1, other arithmetic, body(): up_pre = pre_act[:, 1, :].astype(f32)  4.38 us
    transpose x1, other arithmetic, body(): activation.reshape(row_count, 2, 4, 4, 2, 2, 8)  3.82 us
    convert_element_type x1, local copies, waits for them, and re-layouts, body(): up_pre = pre_act[:, 1, :].astype(f32)  3.62 us
    convert_element_type x1, local copies, waits for them, and re-layouts, body(): gate_pre = pre_act[:, 0, :].astype(f32)  3.57 us

profile of v1, /device:TPU:0, one launch (start us, length us, event | category | flops | bytes accessed | tf_op | source)
XLA Modules:
  0.0 144.0 jit_solution(16215888274893992025)
XLA Ops:
  0.6 8.0 %fusion.12 = (bf16[768,1,1024]{2,1,0:T(2,128)(2,1)S(1)}, bf16[768,1,1024]{2,1,0:T(2,128)(2,1)S(1)}) fusion(bf16[768,2,1024]{2,1,0:T(2,128)(2,1)} %param.6), kind=kLoop, calls=%fused_computation.28 | loop fusion | bytes 6291456 | tf_op jit(solution)/shard_map/slice | solution.py:372
  8.6 0.0 copy-start
  8.6 4.4 %copy_convert_fusion = (f32[768,1,1024]{2,0,1:T(8,128)}, f32[768,1,1024]{2,0,1:T(8,128)}) fusion(bf16[768,1,1024]{2,1,0:T(2,128)(2,1)S(1)} %get-tuple-element.13, bf16[768,1,1024]{2,1,0:T(2,128)(2,1)S(1)} %get-tuple-element.12), kind=kLoop, calls=%fused_computation.16 | loop fusion | flops 1572864 | bytes 9437184 | tf_op jit(solution)/shard_map/convert_element_type | solution.py:373
  13.0 0.0 copy-done
  13.0 3.6 %copy.14 = f32[768,1,1024]{0,2,1:T(8,128)} copy(f32[768,1,1024]{2,0,1:T(8,128)} %get-tuple-element.15) | data formatting | bytes 6291456 | tf_op jit(solution)/shard_map/convert_element_type | solution.py:372
  16.6 0.0 copy-start.4
  16.6 3.6 %copy.16 = f32[768,1,1024]{0,2,1:T(8,128)} copy(f32[768,1,1024]{2,0,1:T(8,128)} %get-tuple-element.14) | data formatting | bytes 6291456 | tf_op jit(solution)/shard_map/convert_element_type | solution.py:373
  20.2 0.0 copy-done.4
  20.2 0.1 convert_bitcast_fusion
  20.3 3.8 %fusion.9 = bf16[2,4,2,2,4,8,768]{6,5,0,2,4,1,3:T(8,128)(2,1)S(1)} fusion(f32[768,2,4,4,2,2,8]{0,6,5,4,3,2,1:T(8,128)} %bitcast.59, f32[768,2,4,4,2,2,8]{0,6,5,4,3,2,1:T(8,128)} %bitcast.58, f32[768]{0:T(1024)S(1)} %convert_bitcast_fusion), kind=kLoop, calls=%fused_computation.18 | loop fusion | flops 5505024 | bytes 7867392 | tf_op jit(solution)/shard_map/transpose | solution.py:377
  24.1 0.2 copy.17
  24.3 0.0 copy-start.3
  24.3 0.2 broadcast_in_dim.44
  24.6 0.4 copy-done.3
  25.0 0.1 broadcast_bitcast_fusion
  25.1 0.0 copy-start.1
  25.1 1.9 %broadcast_select_fusion.lhs_hbm = bf16[2,4,4,64,768]{4,3,2,1,0:T(8,128)(2,1)} fusion(bf16[2,4,4,64,768]{4,3,2,1,0:T(8,128)(2,1)S(1)} %bitcast.60, pred[64,768]{1,0:T(8,128)(4,1)S(1)} %bitcast.64), kind=kLoop, calls=%fused_computation.15 | loop fusion | flops 1572864 | bytes 6340608 | tf_op jit(solution)/shard_map/jit(_where)/select_n | solution.py:379
  27.0 0.0 copy-done.1
  27.0 1.0 copy.33
  28.0 0.1 compare_convert_fusion
  28.1 0.9 broadcast_in_dim.47.hot_ref
  29.0 104.1 %shard_map.68 = (f32[768,1024]{1,0:T(8,128)}, f32[16,3584]{1,0:T(8,128)}) custom-call(bf16[768,3584]{1,0:T(8,128)(2,1)} %cot_hbm.1, bf16[2,4,4,64,768]{4,3,2,1,0:T(8,128)(2,1)} %broadcast_select_fusion.lhs_hbm, bf16[2,64,3584]{2,1,0:T(8,128)(2,1)} %bitcast.61, f32[768,128]{1,0:T(8,128)} %broadcast_in_dim.47.hot_ref), custom_call_target="tpu_custom_call" | custom-call | flops 24000000000 | bytes 30000000 | tf_op jit(solution)/shard_map/pallas_call | solution.py:328
  133.1 4.9 %fusion.11 = (bf16[768,1,1024]{2,0,1:T(8,128)(2,1)S(1)}, bf16[768,1,1024]{2,0,1:T(8,128)(2,1)S(1)}) fusion(f32[768,1024]{1,0:T(8,128)} %get-tuple-element.4, f32[768]{0:T(1024)S(1)} %convert_bitcast_fusion, bf16[768,1,1024]{2,1,0:T(2,128)(2,1)} %copy-done, bf16[768,1,1024]{2,1,0:T(2,128)(2,1)S(1)} %get-tuple-element.12), kind=kLoop, calls=%fused_computation.20 | loop fusion | flops 12582912 | bytes 9440256 | tf_op jit(solution)/shard_map/stack | solution.py:388
  138.0 0.3 pad_maximum_fusion
  138.3 0.0 copy-start.2
  138.3 4.9 %copy.20 = bf16[768,2,1024]{2,1,0:T(2,128)(2,1)} copy(bf16[768,2,1024]{2,0,1:T(8,128)(2,1)S(1)} %pad_maximum_fusion) | data formatting | bytes 6291456
  143.2 0.0 copy-done.2
  143.2 0.9 copy.34
  (2 shorter events, 0.0 us)
Async XLA Ops:
  8.6 4.4 %copy-start = (bf16[768,1,1024]{2,1,0:T(2,128)(2,1)}, bf16[768,1,1024]{2,1,0:T(2,128)(2,1)S(1)}, u32[]{:S(2)}) copy-start(bf16[768,1,1024]{2,1,0:T(2,128)(2,1)S(1)} %get-tuple-element.13) | copy-start | bytes 4718596
  16.6 3.6 %copy-start.4 = (s32[6]{0:T(128)S(1)}, s32[6]{0:T(128)}, u32[]{:S(2)}) copy-start(s32[6]{0:T(128)} %param.9) | copy-start | bytes 76
  24.3 0.7 copy-start.3
  25.1 1.9 %copy-start.1 = (bf16[64,2,3584]{2,1,0:T(2,128)(2,1)S(1)}, bf16[64,2,3584]{2,1,0:T(2,128)(2,1)}, u32[]{:S(2)}) copy-start(bf16[64,2,3584]{2,1,0:T(2,128)(2,1)} %param.7) | copy-start | bytes 2752516
  138.3 4.9 %copy-start.2 = (f32[16,3584]{1,0:T(8,128)S(1)}, f32[16,3584]{1,0:T(8,128)}, u32[]{:S(2)}) copy-start(f32[16,3584]{1,0:T(8,128)} %get-tuple-element.5) | copy-start | bytes 688132

commit v2 on v0

v2 whole, which is shorter than its diff:
```python
import functools

import jax
import jax.numpy as jnp
from jax import lax
from jax.experimental import pallas as pl
from jax.experimental.pallas import tpu as pltpu
from jax.sharding import PartitionSpec as P

MESH = pl.DeviceIdType.MESH
grad_factor = 0.015625

ROWS = 768
HIDDEN = 1024
WIDTH = 3584
WIDE = 512
CHUNKS = WIDTH // WIDE
SPLIT = (384, 128)
STREAM_ROWS = (256, 64)
f32 = jnp.float32
bf16 = jnp.bfloat16

EVENTS = {1: ((1, 0), (2, 1)), 2: ((1, 1), (2, 0)), 3: ((4, 0), (4, 1)), 4: ((3, 0), (3, 1)),
          6: ((5, 0), (6, 1)), 7: ((5, 1), (6, 0)), 9: ((7, 0), (7, 1))}
ORDER = (0, 1, 2, 4, 3, 5, 6, 7)
TURNS = {2: (0,), 3: (1,), 4: (2,), 5: (3,), 6: (4,), 8: (5,), 9: (6,), 11: (7,)}


def kernel(
    cot_hbm, pre_hbm, w_hbm, expert_ref, fill_ref,
    act_hbm, wgrad_hbm,
    cot_own, cot_sib, pre, lhs, lhs_sib, w_all, grad_buf, out_buf, mixed,
    rings, tot,
    cot_sem, pre_sem, w_sem, grad_sem, out_sem,
    cs_send, cs_recv, ls_send, ls_recv,
    ag_send, ag_recv, sib_send, sib_recv,
):
    g = lax.axis_index("group")
    b = lax.axis_index("blk")
    x_lo, z = lax.div(g, 4), lax.rem(g, 4)
    y, c = lax.div(b, 4), lax.rem(b, 2)
    x_hi = lax.rem(lax.div(b, 2), 2)
    x = x_hi * 2 + x_lo

    def device(dx, dy, dz, core):
        xx, yy, zz = lax.rem(x + dx, 4), lax.rem(y + dy, 4), lax.rem(z + dz, 4)
        return (lax.rem(xx, 2) * 4 + zz, yy * 4 + lax.div(xx, 2) * 2 + core)

    other = 1 - c
    sibling = device(0, 0, 0, other)
    x_up, x_dn = device(1, 0, 0, c), device(3, 0, 0, c)
    y_up, y_dn = device(0, 1, 0, c), device(0, 3, 0, c)
    z_up, z_dn = device(0, 0, 1, c), device(0, 0, 3, c)
    x_peer = device(3 - 2 * x + 4, 0, 0, c)

    barrier = pltpu.get_barrier_semaphore()
    for peer in (sibling, x_up, x_dn, y_up, y_dn, z_up, z_dn):
        pl.semaphore_signal(barrier, inc=1, device_id=peer, device_id_type=MESH)

    def cot_cols(k):
        return pl.ds(pl.multiple_of(k * WIDE, WIDE), WIDE)

    def cot_copy(k):
        return pltpu.make_async_copy(cot_hbm.at[:, cot_cols(k)], cot_own.at[:, cot_cols(k)], cot_sem.at[k])

    def pre_copy():
        return pltpu.make_async_copy(pre_hbm, pre, pre_sem)

    q_own = y * 2 + x_hi

    def w_copy(e):
        return pltpu.make_async_copy(w_hbm.at[e], w_all.at[q_own, e, c], w_sem.at[e])

    for e in range(2):
        w_copy(e).start()
    pre_copy().start()

    @pl.loop(0, CHUNKS)
    def _(k):
        cot_copy(k).start()

    pl.semaphore_wait(barrier, 7)

    def remote(src, dst, send, recv, device_id):
        return pltpu.make_async_remote_copy(
            src_ref=src, dst_ref=dst, send_sem=send, recv_sem=recv, device_id=device_id, device_id_type=MESH
        )

    def lhs_remote():
        return remote(lhs.at[1], lhs_sib, ls_send, ls_recv, sibling)

    def cot_remote(k):
        return remote(
            cot_hbm.at[:, cot_cols(k)], cot_sib.at[:, cot_cols(k)], cs_send.at[k], cs_recv.at[k], sibling
        )

    def piece(j):
        yy = lax.rem(y + (0, 3, 1, 2)[j % 4], 4)
        return yy * 2 + (x_hi if j < 4 else 1 - x_hi)

    def gather(slot):
        src_j, dst_j, e, device_id = sends[slot]
        block = w_all.at[piece(src_j), e, c]
        return remote(block, block, ag_send.at[slot], ag_recv.at[dst_j, e], device_id)

    def gather_wait(j, e):
        block = w_all.at[piece(j), e, c]
        remote(block, block, ag_send.at[0], ag_recv.at[j, e], sibling).wait_recv()

    def share(j, e):
        block = w_all.at[piece(j), e, c]
        return remote(block, block, sib_send.at[j, e], sib_recv.at[j, e], sibling)

    def share_wait(j, e):
        block = w_all.at[piece(j), e, other]
        remote(block, block, sib_send.at[j, e], sib_recv.at[j, e], sibling).wait_recv()

    sends = [(0, 1, 0, y_up), (0, 2, 1, y_dn), (0, 4, 0, x_peer), (0, 4, 1, x_peer), (0, 1, 1, y_up), (0, 2, 0, y_dn)]
    sends += [(1, 3, 0, y_up), (2, 3, 1, y_dn)]
    for e in range(2):
        sends += [(4, 5, e, y_up), (4, 6, e, y_dn)]
    sends += [(5, 7, 0, y_up), (6, 7, 1, y_dn)]

    def gather_start(j, e):
        for slot, (src_j, _, src_e, _) in enumerate(sends):
            if (src_j, src_e) == (j, e):
                gather(slot).start()

    def arrived(j, e):
        gather_wait(j, e)
        gather_start(j, e)
        share(j, e).start()

    cot_remote(0).start()
    for e in range(2):
        w_copy(e).wait()
    for slot in range(6):
        gather(slot).start()

    @pl.loop(1, CHUNKS)
    def _(k):
        cot_remote(k).start()

    pre_copy().wait()

    @pl.loop(0, ROWS // 128)
    def _(t):
        rows = pl.ds(pl.multiple_of(t * 128, 128), 128)
        lane = lax.broadcasted_iota(jnp.int32, (8, 128), 1)
        alive = lane < fill_ref[t]
        chosen = jnp.zeros((8, 128), jnp.int32) + expert_ref[t]
        masks = [jnp.logical_and(alive, chosen == e) for e in range(2)]

        @pl.loop(0, 8)
        def _(part):
            cols = pl.ds(pl.multiple_of(part * 128, 128), 128)
            gate = pre[0, rows, cols].astype(f32)
            up = pre[1, rows, cols].astype(f32)
            sig = 1.0 / (1.0 + jnp.exp(-gate))
            turned = jnp.transpose(gate * sig * up)
            part_x, part_z = lax.div(part, 4), lax.rem(part, 4)
            for yy in range(4):
                for hi in range(2):
                    for core in range(2):
                        at = yy * 32 + hi * 16 + core * 8
                        value = turned[at:at + 8]
                        pair = jnp.concatenate([jnp.where(mask, value, 0.0) for mask in masks], axis=0)
                        lhs[lax.rem(c + core, 2), part_z, hi * 2 + part_x, yy * 16:yy * 16 + 16, rows] = pair.astype(bf16)

    lhs_remote().start()
    for e in range(2):
        share(0, e).start()

    z_ring, x_ring, y_ring = (z, z_up, z_dn), (x, x_up, x_dn), (y, y_up, y_dn)
    ring_of = ((z_ring, x_ring), (x_ring, z_ring), (y_ring,))

    def far_copy(st, s, k, half):
        far, rfar, send, recv = (rings[st][s][i] for i in (0, 3, 8, 9))
        rows = far.shape[1] // 2
        return remote(
            far.at[k, pl.ds(half * rows, rows)], rfar.at[k, pl.ds(half * rows, rows)],
            send.at[k, half], recv.at[k, half], ring_of[st][s][1 + half],
        )

    def near_copy(st, s, k, way):
        src, dst, send, recv = (rings[st][s][i] for i in (1 + way, 4 + way, 8, 9))
        return remote(src.at[k], dst.at[k], send.at[k, 2 + way], recv.at[k, 2 + way], ring_of[st][s][1 + way])

    def emit(st, s, k, offset, value):
        far, up, dn, _, _, _, own, rel, _, _ = rings[st][s]
        half = far.shape[1] // 2
        kind = far.dtype
        if offset == 2:
            far[k] = value.astype(kind)
            far_copy(st, s, k, 0).start()
            far_copy(st, s, k, 1).start()
        elif offset == 1:
            rel[lax.rem(k, 2), 0] = value[:half]
            up[k, half:] = value[half:].astype(kind)
        elif offset == 3:
            rel[lax.rem(k, 2), 1] = value[half:]
            dn[k, :half] = value[:half].astype(kind)
        else:
            own[lax.rem(k, 4)] = value

    def relay(st, s, k):
        _, up, dn, rfar, _, _, _, rel, _, _ = rings[st][s]
        half = up.shape[1] // 2
        kind = up.dtype
        far_copy(st, s, k, 0).wait_recv()
        up[k, :half] = (rel[lax.rem(k, 2), 0] + rfar[k, :half].astype(f32)).astype(kind)
        near_copy(st, s, k, 0).start()
        far_copy(st, s, k, 1).wait_recv()
        dn[k, half:] = (rel[lax.rem(k, 2), 1] + rfar[k, half:].astype(f32)).astype(kind)
        near_copy(st, s, k, 1).start()

    def total(st, s, k):
        near_copy(st, s, k, 0).wait_recv()
        near_copy(st, s, k, 1).wait_recv()
        _, _, _, _, rup, rdn, own, _, _, _ = rings[st][s]
        return own[lax.rem(k, 4)] + rup[k].astype(f32) + rdn[k].astype(f32)

    def make(k):
        cot_remote(k).wait_recv()
        cols = cot_cols(k)
        for offset in (2, 1, 3, 0):
            at = lax.rem(z + offset, 4)
            value = jnp.dot(lhs[0, at].reshape(256, ROWS), cot_own[:, cols], preferred_element_type=f32)
            value += jnp.dot(lhs_sib[at].reshape(256, ROWS), cot_sib[:, cols], preferred_element_type=f32)
            emit(0, 0, k, offset, value[:, :SPLIT[0]])
            mixed[at] = value[:, SPLIT[0]:].reshape(4, 64, SPLIT[1])
        for offset in (2, 1, 3, 0):
            at = lax.rem(x + offset, 4)
            emit(1, 0, k, offset, mixed[:, at].reshape(256, SPLIT[1]))

    def onward(k):
        for st in range(2):
            tot[st][...] = total(st, 0, k)
            me = ring_of[st][1][0]
            for offset in (2, 1, 3, 0):
                at = pl.multiple_of(lax.rem(me + offset, 4) * 64, 64)
                emit(st, 1, k, offset, tot[st][pl.ds(at, 64), :])

    def joined(k):
        for st in range(2):
            tot[2][:, st * SPLIT[0]:st * SPLIT[0] + SPLIT[st]] = total(st, 1, k)
        for offset in (2, 1, 3, 0):
            at = pl.multiple_of(lax.rem(y + offset, 4) * 16, 16)
            emit(2, 0, k, offset, tot[2][pl.ds(at, 16), :])

    def last(k):
        out_buf[:, cot_cols(k)] = total(2, 0, k) * grad_factor

    def grad_copy(turn):
        cols = pl.ds(pl.multiple_of(piece(ORDER[turn]) * 128, 128), 128)
        return pltpu.make_async_copy(grad_buf.at[turn % 2], act_hbm.at[:, :, cols], grad_sem.at[turn])

    def hidden(turn):
        j = ORDER[turn]
        for e in range(2):
            share_wait(j, e)
        if turn >= 2:
            grad_copy(turn - 2).wait()
        q = piece(j)
        cols = pl.ds(pl.multiple_of(q * 128, 128), 128)

        @pl.loop(0, ROWS // 256)
        def _(m):
            rows = pl.ds(pl.multiple_of(m * 256, 256), 256)
            each = lax.dot_general(
                cot_own[rows, :], w_all[q].reshape(256, WIDTH), (((1,), (1,)), ((), ())), preferred_element_type=f32
            )
            for i in range(2):
                part = pl.ds(pl.multiple_of(m * 256 + i * 128, 128), 128)
                row = lax.broadcasted_iota(jnp.int32, (128, 128), 0)
                alive = row < fill_ref[m * 2 + i]
                second = jnp.zeros((128, 128), jnp.int32) + expert_ref[m * 2 + i] == 1
                both = each[i * 128:(i + 1) * 128]
                grad = jnp.where(alive, jnp.where(second, both[:, 128:], both[:, :128]), 0.0)
                gate = pre[0, part, cols].astype(f32)
                up = pre[1, part, cols].astype(f32)
                sig = 1.0 / (1.0 + jnp.exp(-gate))
                grad_buf[turn % 2, 0, part, :] = (grad * up * sig * (1.0 + gate * (1.0 - sig))).astype(bf16)
                grad_buf[turn % 2, 1, part, :] = (grad * (gate * sig)).astype(bf16)

        grad_copy(turn).start()

    @pl.loop(0, CHUNKS)
    def _(k):
        cot_copy(k).wait()

    lhs_remote().wait_recv()

    @pl.loop(0, CHUNKS + 6)
    def _(t):
        def at(lag, do):
            @pl.when(jnp.logical_and(t >= lag, t < CHUNKS + lag))
            def _():
                do(t - lag)

        def on(when, do):
            @pl.when(t == when)
            def _():
                do()

        def both(do, s):
            def run(k):
                for st in range(2):
                    do(st, s, k)

            return run

        for when, those in EVENTS.items():
            for j, e in those:
                on(when, functools.partial(arrived, j, e))
        at(0, make)
        at(1, both(relay, 0))
        at(2, onward)
        at(3, both(relay, 1))
        at(4, joined)
        at(5, functools.partial(relay, 2, 0))
        at(6, last)

        for when, those in TURNS.items():
            for turn in those:
                on(when, functools.partial(hidden, turn))

    out = pltpu.make_async_copy(out_buf, wgrad_hbm, out_sem)
    out.start()
    for turn in (6, 7):
        grad_copy(turn).wait()
    out.wait()

    lhs_remote().wait_send()

    @pl.loop(0, CHUNKS)
    def _(k):
        cot_remote(k).wait_send()
        for st, s in ((0, 0), (0, 1), (1, 0), (1, 1), (2, 0)):
            for i in range(2):
                far_copy(st, s, k, i).wait_send()
                near_copy(st, s, k, i).wait_send()

    for slot in range(len(sends)):
        gather(slot).wait_send()
    for j in range(8):
        for e in range(2):
            share(j, e).wait_send()


def ring_scratch(rows, cols, kind):
    dma = pltpu.SemaphoreType.DMA
    return (
        *[pltpu.VMEM((CHUNKS, rows, cols), kind)] * 6,
        pltpu.VMEM((4, rows, cols), f32),
        pltpu.VMEM((2, 2, rows // 2, cols), f32),
        dma((CHUNKS, 4)),
        dma((CHUNKS, 4)),
    )


def call(cot, pre, w, expert, fill):
    dma = pltpu.SemaphoreType.DMA
    any_space = pl.BlockSpec(memory_space=pl.ANY)
    scalars = pl.BlockSpec(memory_space=pltpu.SMEM)
    return pl.pallas_call(
        kernel,
        out_shape=(
            jax.ShapeDtypeStruct((2, ROWS, HIDDEN), bf16),
            jax.ShapeDtypeStruct((16, WIDTH), f32),
        ),
        in_specs=[any_space, any_space, any_space, scalars, scalars],
        out_specs=(any_space, any_space),
        scratch_shapes=[
            pltpu.VMEM((ROWS, WIDTH), bf16),
            pltpu.VMEM((ROWS, WIDTH), bf16),
            pltpu.VMEM((2, ROWS, HIDDEN), bf16),
            pltpu.VMEM((2, 4, 4, 64, ROWS), bf16),
            pltpu.VMEM((4, 4, 64, ROWS), bf16),
            pltpu.VMEM((8, 2, 2, 64, WIDTH), bf16),
            pltpu.VMEM((2, 2, ROWS, 128), bf16),
            pltpu.VMEM((16, WIDTH), f32),
            pltpu.VMEM((4, 4, 64, SPLIT[1]), f32),
            (
                tuple(ring_scratch(r, SPLIT[0], bf16) for r in STREAM_ROWS),
                tuple(ring_scratch(r, SPLIT[1], bf16) for r in STREAM_ROWS),
                (ring_scratch(16, WIDE, f32),),
            ),
            (pltpu.VMEM((256, SPLIT[0]), f32), pltpu.VMEM((256, SPLIT[1]), f32), pltpu.VMEM((64, WIDE), f32)),
            dma((CHUNKS,)), dma, dma((2,)), dma((8,)), dma,
            dma((CHUNKS,)), dma((CHUNKS,)), dma, dma,
            dma((14,)), dma((8, 2)), dma((8, 2)), dma((8, 2)),
        ],
        compiler_params=pltpu.CompilerParams(
            collective_id=0, has_side_effects=True, vmem_limit_bytes=60 * 2**20
        ),
        cost_estimate=pl.CostEstimate(flops=24 * 10**9, bytes_accessed=30 * 10**6, transcendentals=0),
    )(cot, pre, w, expert, fill)


def body(cotangent, pre_act, down_weight, tile_expert, tile_fill):
    act_grad, partial = call(
        cotangent, jnp.swapaxes(pre_act, 0, 1), jnp.swapaxes(down_weight, 0, 1), tile_expert, tile_fill
    )
    return jnp.swapaxes(act_grad, 0, 1), jnp.swapaxes(partial.reshape(2, 8, WIDTH), 0, 1)


def solution(mesh):
    placed = (
        P(("group", "blk"), None),
        P(("group", "blk"), None, None),
        P("blk", None, None),
        P(("group", "blk")),
        P(("group", "blk")),
    )
    return jax.shard_map(
        body,
        mesh=mesh,
        in_specs=placed,
        out_specs=(P(("group", "blk"), None, None), P(("group", "blk"), None, None)),
        check_vma=False,
    )
```

time: 381 us -> 108 us (0.28)
  waiting for transfers between devices: 188 us -> 0 us
  local copies, waits for them, and re-layouts: 132 us -> 14.4 us
  Pallas kernels: 0 us -> 92.8 us
  matrix products: 38.3 us -> 0 us
  between operations: 13.9 us -> 0.65 us
  other arithmetic: 5.99 us -> 0 us
    reduce_scatter x2 -> x0, waiting for transfers between devices: 134 us -> none  [the longest x1 125 us: body(): lax.psum_scatter(jnp.einsum('treh,trd->hed', act_expert, cot_tiles, prefe...]
    pallas_call x0 -> x1, Pallas kernels: none -> 92.8 us  [call(): pl.pallas_call(kernel, out_shape=(jax.ShapeDtypeStruct((2, ROWS, HIDDEN),...]
    all_gather x1 -> x0, waiting for transfers between devices: 53 us -> none  [body(): piece = lax.all_gather(down_weight, 'blk', axis=0, tiled=True)]
    gather x5 -> x0, local copies, waits for them, and re-layouts: 49.8 us -> none  [body(): chosen = jnp.take(piece, tile_expert, axis=1)]
    unnamed x24 -> x5, local copies, waits for them, and re-layouts: 62 us -> 13.5 us
    dot_general x2 -> x0, matrix products: 38.3 us -> none  [the longest x1 19.7 us: body(): jnp.einsum('trd,ntd->trn', cot_tiles, chosen, preferred_element_type=jnp....]
    slice x1 -> x0, local copies, waits for them, and re-layouts: 9.44 us -> none  [body(): up_pre = pre_act[:, 1, :].astype(jnp.float32)]
    broadcast_in_dim x2 -> x0, local copies, waits for them, and re-layouts: 6.12 us -> none  [body(): jnp.where(expert_hot[:, None, :, None], reordered, jnp.zeros((), jnp.bflo...]
  transfers between devices with their start and end apart: 3 -> 0, of which waited for: 3 -> 0; matrix products, arithmetic and copies ran while one was open for 46% -> 0% of each run, Pallas kernels for 0% -> 0%
where the time goes in v2:
time: 108 us
  Pallas kernels  92.8 us (86%)
  local copies, waits for them, and re-layouts  14.4 us (13%)
    pallas_call x1, Pallas kernels, call(): pl.pallas_call(kernel, out_shape=(jax.ShapeDtypeStruct((2, ROWS, HIDDEN),...  92.8 us
    unnamed x5, local copies, waits for them, and re-layouts  13.5 us

profile of v2, /device:TPU:0, one launch (start us, length us, event | category | flops | bytes accessed | tf_op | source)
XLA Modules:
  0.0 107.9 jit_solution(10503985555000203421)
XLA Ops:
  0.6 2.2 %copy.15 = bf16[64,2,3584]{2,0,1:T(8,128)(2,1)} copy(bf16[64,2,3584]{2,1,0:T(2,128)(2,1)} %param.7) | data formatting | bytes 1835008 | tf_op args[2]
  2.8 4.5 %copy.14 = bf16[768,2,1024]{2,0,1:T(8,128)(2,1)} copy(bf16[768,2,1024]{2,1,0:T(2,128)(2,1)} %param.6) | data formatting | bytes 6291456 | tf_op args[1]
  7.3 92.8 %shard_map.68 = (bf16[2,768,1024]{2,1,0:T(8,128)(2,1)}, f32[16,3584]{1,0:T(8,128)}) custom-call(bf16[768,3584]{1,0:T(8,128)(2,1)} %cot_hbm.1, bf16[2,768,1024]{2,1,0:T(8,128)(2,1)} %bitcast.12, bf16[2,64,3584]{2,1,0:T(8,128)(2,1)} %bitcast.13, s32[6]{0:T(128)} %expert_ref.1, s32[6]{0:T(128)} %fill_ref.1), custom_call_target="tpu_custom_call" | custom-call | flops 24000000000 | bytes 30000000 | tf_op jit(solution)/shard_map/pallas_call | solution.py:366
  100.2 0.0 copy-start
  100.2 6.8 %copy.10 = bf16[768,2,1024]{2,1,0:T(2,128)(2,1)} copy(bf16[768,2,1024]{2,0,1:T(8,128)(2,1)} %bitcast.11) | data formatting | bytes 6291456
  107.0 0.0 copy-done
  107.0 0.9 copy.16
Async XLA Ops:
  100.2 6.8 %copy-start = (f32[16,3584]{1,0:T(8,128)S(1)}, f32[16,3584]{1,0:T(8,128)}, u32[]{:S(2)}) copy-start(f32[16,3584]{1,0:T(8,128)} %get-tuple-element.5) | copy-start | bytes 688132

commit v3 on v2

--- a/solution.py
+++ b/solution.py
@@ -16,21 +16,20 @@
 WIDE = 512
 CHUNKS = WIDTH // WIDE
 SPLIT = (384, 128)
-STREAM_ROWS = (256, 64)
 f32 = jnp.float32
 bf16 = jnp.bfloat16
 
-EVENTS = {1: ((1, 0), (2, 1)), 2: ((1, 1), (2, 0)), 3: ((4, 0), (4, 1)), 4: ((3, 0), (3, 1)),
-          6: ((5, 0), (6, 1)), 7: ((5, 1), (6, 0)), 9: ((7, 0), (7, 1))}
+EVENTS = {1: ((1, 0), (2, 1)), 2: ((1, 1), (2, 0), (4, 0), (4, 1)), 4: ((3, 0), (3, 1)),
+          5: ((5, 0), (6, 1)), 7: ((5, 1), (6, 0)), 10: ((7, 0), (7, 1))}
 ORDER = (0, 1, 2, 4, 3, 5, 6, 7)
-TURNS = {2: (0,), 3: (1,), 4: (2,), 5: (3,), 6: (4,), 8: (5,), 9: (6,), 11: (7,)}
+TURNS = {2: (0,), 3: (1,), 4: (2,), 5: (3,), 6: (4,), 8: (5,), 9: (6,), 10: (7,)}
 
 
 def kernel(
     cot_hbm, pre_hbm, w_hbm, expert_ref, fill_ref,
     act_hbm, wgrad_hbm,
     cot_own, cot_sib, pre, lhs, lhs_sib, w_all, grad_buf, out_buf, mixed,
-    rings, tot,
+    rings, directs, tot,
     cot_sem, pre_sem, w_sem, grad_sem, out_sem,
     cs_send, cs_recv, ls_send, ls_recv,
     ag_send, ag_recv, sib_send, sib_recv,
@@ -51,10 +50,11 @@
     x_up, x_dn = device(1, 0, 0, c), device(3, 0, 0, c)
     y_up, y_dn = device(0, 1, 0, c), device(0, 3, 0, c)
     z_up, z_dn = device(0, 0, 1, c), device(0, 0, 3, c)
+    x_far, y_far, z_far = device(2, 0, 0, c), device(0, 2, 0, c), device(0, 0, 2, c)
     x_peer = device(3 - 2 * x + 4, 0, 0, c)
 
     barrier = pltpu.get_barrier_semaphore()
-    for peer in (sibling, x_up, x_dn, y_up, y_dn, z_up, z_dn):
+    for peer in (sibling, x_up, x_dn, x_far, y_up, y_dn, y_far, z_up, z_dn, z_far):
         pl.semaphore_signal(barrier, inc=1, device_id=peer, device_id_type=MESH)
 
     def cot_cols(k):
@@ -79,15 +79,18 @@
     def _(k):
         cot_copy(k).start()
 
-    pl.semaphore_wait(barrier, 7)
+    pl.semaphore_wait(barrier, 10)
 
     def remote(src, dst, send, recv, device_id):
         return pltpu.make_async_remote_copy(
             src_ref=src, dst_ref=dst, send_sem=send, recv_sem=recv, device_id=device_id, device_id_type=MESH
         )
 
-    def lhs_remote():
-        return remote(lhs.at[1], lhs_sib, ls_send, ls_recv, sibling)
+    def lhs_remote(t):
+        rows = pl.ds(pl.multiple_of(t * 128, 128), 128)
+        return remote(
+            lhs.at[1, :, :, :, rows], lhs_sib.at[:, :, :, rows], ls_send.at[t], ls_recv.at[t], sibling
+        )
 
     def cot_remote(k):
         return remote(
@@ -136,10 +139,6 @@
         w_copy(e).wait()
     for slot in range(6):
         gather(slot).start()
-
-    @pl.loop(1, CHUNKS)
-    def _(k):
-        cot_remote(k).start()
 
     pre_copy().wait()
 
@@ -167,33 +166,39 @@
                         pair = jnp.concatenate([jnp.where(mask, value, 0.0) for mask in masks], axis=0)
                         lhs[lax.rem(c + core, 2), part_z, hi * 2 + part_x, yy * 16:yy * 16 + 16, rows] = pair.astype(bf16)
 
-    lhs_remote().start()
+        lhs_remote(t).start()
+
+    @pl.loop(1, CHUNKS)
+    def _(k):
+        cot_remote(k).start()
+
     for e in range(2):
         share(0, e).start()
 
-    z_ring, x_ring, y_ring = (z, z_up, z_dn), (x, x_up, x_dn), (y, y_up, y_dn)
-    ring_of = ((z_ring, x_ring), (x_ring, z_ring), (y_ring,))
-
-    def far_copy(st, s, k, half):
-        far, rfar, send, recv = (rings[st][s][i] for i in (0, 3, 8, 9))
+    z_ring, x_ring, y_ring = (z, z_up, z_dn, z_far), (x, x_up, x_dn, x_far), (y, y_up, y_dn, y_far)
+    ring_of = (z_ring, x_ring)
+    direct_of = (x_ring, z_ring, y_ring)
+
+    def far_copy(st, k, half):
+        far, rfar, send, recv = (rings[st][i] for i in (0, 3, 8, 9))
         rows = far.shape[1] // 2
         return remote(
             far.at[k, pl.ds(half * rows, rows)], rfar.at[k, pl.ds(half * rows, rows)],
-            send.at[k, half], recv.at[k, half], ring_of[st][s][1 + half],
+            send.at[k, half], recv.at[k, half], ring_of[st][1 + half],
         )
 
-    def near_copy(st, s, k, way):
-        src, dst, send, recv = (rings[st][s][i] for i in (1 + way, 4 + way, 8, 9))
-        return remote(src.at[k], dst.at[k], send.at[k, 2 + way], recv.at[k, 2 + way], ring_of[st][s][1 + way])
-
-    def emit(st, s, k, offset, value):
-        far, up, dn, _, _, _, own, rel, _, _ = rings[st][s]
+    def near_copy(st, k, way):
+        src, dst, send, recv = (rings[st][i] for i in (1 + way, 4 + way, 8, 9))
+        return remote(src.at[k], dst.at[k], send.at[k, 2 + way], recv.at[k, 2 + way], ring_of[st][1 + way])
+
+    def emit(st, k, offset, value):
+        far, up, dn, _, _, _, own, rel, _, _ = rings[st]
         half = far.shape[1] // 2
         kind = far.dtype
         if offset == 2:
             far[k] = value.astype(kind)
-            far_copy(st, s, k, 0).start()
-            far_copy(st, s, k, 1).start()
+            far_copy(st, k, 0).start()
+            far_copy(st, k, 1).start()
         elif offset == 1:
             rel[lax.rem(k, 2), 0] = value[:half]
             up[k, half:] = value[half:].astype(kind)
@@ -203,22 +208,40 @@
         else:
             own[lax.rem(k, 4)] = value
 
-    def relay(st, s, k):
-        _, up, dn, rfar, _, _, _, rel, _, _ = rings[st][s]
-        half = up.shape[1] // 2
-        kind = up.dtype
-        far_copy(st, s, k, 0).wait_recv()
-        up[k, :half] = (rel[lax.rem(k, 2), 0] + rfar[k, :half].astype(f32)).astype(kind)
-        near_copy(st, s, k, 0).start()
-        far_copy(st, s, k, 1).wait_recv()
-        dn[k, half:] = (rel[lax.rem(k, 2), 1] + rfar[k, half:].astype(f32)).astype(kind)
-        near_copy(st, s, k, 1).start()
-
-    def total(st, s, k):
-        near_copy(st, s, k, 0).wait_recv()
-        near_copy(st, s, k, 1).wait_recv()
-        _, _, _, _, rup, rdn, own, _, _, _ = rings[st][s]
+    def relay(k):
+        for st in range(2):
+            _, up, dn, rfar, _, _, _, rel, _, _ = rings[st]
+            half = up.shape[1] // 2
+            kind = up.dtype
+            far_copy(st, k, 0).wait_recv()
+            up[k, :half] = (rel[lax.rem(k, 2), 0] + rfar[k, :half].astype(f32)).astype(kind)
+            near_copy(st, k, 0).start()
+            far_copy(st, k, 1).wait_recv()
+            dn[k, half:] = (rel[lax.rem(k, 2), 1] + rfar[k, half:].astype(f32)).astype(kind)
+            near_copy(st, k, 1).start()
+
+    def total(st, k):
+        near_copy(st, k, 0).wait_recv()
+        near_copy(st, k, 1).wait_recv()
+        _, _, _, _, rup, rdn, own, _, _, _ = rings[st]
         return own[lax.rem(k, 4)] + rup[k].astype(f32) + rdn[k].astype(f32)
+
+    def direct_copy(st, k, i):
+        out, came, _, send, recv = directs[st]
+        return remote(out.at[k, i], came.at[k, i], send.at[k, i], recv.at[k, i], direct_of[st][1 + i])
+
+    def spread(st, k, load):
+        out, _, own, _, _ = directs[st]
+        for i, offset in ((2, 2), (0, 1), (1, 3)):
+            out[k, i] = load(lax.rem(direct_of[st][0] + offset, 4)).astype(out.dtype)
+            direct_copy(st, k, i).start()
+        own[lax.rem(k, 2)] = load(direct_of[st][0])
+
+    def collected(st, k):
+        _, came, own, _, _ = directs[st]
+        for i in range(3):
+            direct_copy(st, k, i).wait_recv()
+        return own[lax.rem(k, 2)] + came[k, 0].astype(f32) + came[k, 1].astype(f32) + came[k, 2].astype(f32)
 
     def make(k):
         cot_remote(k).wait_recv()
@@ -227,29 +250,24 @@
             at = lax.rem(z + offset, 4)
             value = jnp.dot(lhs[0, at].reshape(256, ROWS), cot_own[:, cols], preferred_element_type=f32)
             value += jnp.dot(lhs_sib[at].reshape(256, ROWS), cot_sib[:, cols], preferred_element_type=f32)
-            emit(0, 0, k, offset, value[:, :SPLIT[0]])
+            emit(0, k, offset, value[:, :SPLIT[0]])
             mixed[at] = value[:, SPLIT[0]:].reshape(4, 64, SPLIT[1])
         for offset in (2, 1, 3, 0):
             at = lax.rem(x + offset, 4)
-            emit(1, 0, k, offset, mixed[:, at].reshape(256, SPLIT[1]))
+            emit(1, k, offset, mixed[:, at].reshape(256, SPLIT[1]))
 
     def onward(k):
         for st in range(2):
-            tot[st][...] = total(st, 0, k)
-            me = ring_of[st][1][0]
-            for offset in (2, 1, 3, 0):
-                at = pl.multiple_of(lax.rem(me + offset, 4) * 64, 64)
-                emit(st, 1, k, offset, tot[st][pl.ds(at, 64), :])
+            tot[st][...] = total(st, k)
+            spread(st, k, lambda at: tot[st][pl.ds(pl.multiple_of(at * 64, 64), 64), :])
 
     def joined(k):
         for st in range(2):
-            tot[2][:, st * SPLIT[0]:st * SPLIT[0] + SPLIT[st]] = total(st, 1, k)
-        for offset in (2, 1, 3, 0):
-            at = pl.multiple_of(lax.rem(y + offset, 4) * 16, 16)
-            emit(2, 0, k, offset, tot[2][pl.ds(at, 16), :])
+            tot[2][:, st * SPLIT[0]:st * SPLIT[0] + SPLIT[st]] = collected(st, k)
+        spread(2, k, lambda at: tot[2][pl.ds(pl.multiple_of(at * 16, 16), 16), :])
 
     def last(k):
-        out_buf[:, cot_cols(k)] = total(2, 0, k) * grad_factor
+        out_buf[:, cot_cols(k)] = collected(2, k) * grad_factor
 
     def grad_copy(turn):
         cols = pl.ds(pl.multiple_of(piece(ORDER[turn]) * 128, 128), 128)
@@ -280,8 +298,8 @@
                 gate = pre[0, part, cols].astype(f32)
                 up = pre[1, part, cols].astype(f32)
                 sig = 1.0 / (1.0 + jnp.exp(-gate))
-                grad_buf[turn % 2, 0, part, :] = (grad * up * sig * (1.0 + gate * (1.0 - sig))).astype(bf16)
-                grad_buf[turn % 2, 1, part, :] = (grad * (gate * sig)).astype(bf16)
+                grad_buf[turn % 2, part, 0, :] = (grad * up * sig * (1.0 + gate * (1.0 - sig))).astype(bf16)
+                grad_buf[turn % 2, part, 1, :] = (grad * (gate * sig)).astype(bf16)
 
         grad_copy(turn).start()
 
@@ -289,9 +307,11 @@
     def _(k):
         cot_copy(k).wait()
 
-    lhs_remote().wait_recv()
-
-    @pl.loop(0, CHUNKS + 6)
+    @pl.loop(0, ROWS // 128)
+    def _(t):
+        lhs_remote(t).wait_recv()
+
+    @pl.loop(0, CHUNKS + 4)
     def _(t):
         def at(lag, do):
             @pl.when(jnp.logical_and(t >= lag, t < CHUNKS + lag))
@@ -303,23 +323,14 @@
             def _():
                 do()
 
-        def both(do, s):
-            def run(k):
-                for st in range(2):
-                    do(st, s, k)
-
-            return run
-
         for when, those in EVENTS.items():
             for j, e in those:
                 on(when, functools.partial(arrived, j, e))
         at(0, make)
-        at(1, both(relay, 0))
+        at(1, relay)
         at(2, onward)
-        at(3, both(relay, 1))
-        at(4, joined)
-        at(5, functools.partial(relay, 2, 0))
-        at(6, last)
+        at(3, joined)
+        at(4, last)
 
         for when, those in TURNS.items():
             for turn in those:
@@ -331,15 +342,20 @@
         grad_copy(turn).wait()
     out.wait()
 
-    lhs_remote().wait_send()
+    @pl.loop(0, ROWS // 128)
+    def _(t):
+        lhs_remote(t).wait_send()
 
     @pl.loop(0, CHUNKS)
     def _(k):
         cot_remote(k).wait_send()
-        for st, s in ((0, 0), (0, 1), (1, 0), (1, 1), (2, 0)):
+        for st in range(2):
             for i in range(2):
-                far_copy(st, s, k, i).wait_send()
-                near_copy(st, s, k, i).wait_send()
+                far_copy(st, k, i).wait_send()
+                near_copy(st, k, i).wait_send()
+        for st in range(3):
+            for i in range(3):
+                direct_copy(st, k, i).wait_send()
 
     for slot in range(len(sends)):
         gather(slot).wait_send()
@@ -359,6 +375,17 @@
     )
 
 
+def direct_scratch(rows, cols, kind):
+    dma = pltpu.SemaphoreType.DMA
+    return (
+        pltpu.VMEM((CHUNKS, 3, rows, cols), kind),
+        pltpu.VMEM((CHUNKS, 3, rows, cols), kind),
+        pltpu.VMEM((2, rows, cols), f32),
+        dma((CHUNKS, 3)),
+        dma((CHUNKS, 3)),
+    )
+
+
 def call(cot, pre, w, expert, fill):
     dma = pltpu.SemaphoreType.DMA
     any_space = pl.BlockSpec(memory_space=pl.ANY)
@@ -366,7 +393,7 @@
     return pl.pallas_call(
         kernel,
         out_shape=(
-            jax.ShapeDtypeStruct((2, ROWS, HIDDEN), bf16),
+            jax.ShapeDtypeStruct((ROWS, 2, HIDDEN), bf16),
             jax.ShapeDtypeStruct((16, WIDTH), f32),
         ),
         in_specs=[any_space, any_space, any_space, scalars, scalars],
@@ -378,17 +405,18 @@
             pltpu.VMEM((2, 4, 4, 64, ROWS), bf16),
             pltpu.VMEM((4, 4, 64, ROWS), bf16),
             pltpu.VMEM((8, 2, 2, 64, WIDTH), bf16),
-            pltpu.VMEM((2, 2, ROWS, 128), bf16),
+            pltpu.VMEM((2, ROWS, 2, 128), bf16),
             pltpu.VMEM((16, WIDTH), f32),
             pltpu.VMEM((4, 4, 64, SPLIT[1]), f32),
+            tuple(ring_scratch(256, cols, bf16) for cols in SPLIT),
             (
-                tuple(ring_scratch(r, SPLIT[0], bf16) for r in STREAM_ROWS),
-                tuple(ring_scratch(r, SPLIT[1], bf16) for r in STREAM_ROWS),
-                (ring_scratch(16, WIDE, f32),),
+                direct_scratch(64, SPLIT[0], bf16),
+                direct_scratch(64, SPLIT[1], bf16),
+                direct_scratch(16, WIDE, f32),
             ),
             (pltpu.VMEM((256, SPLIT[0]), f32), pltpu.VMEM((256, SPLIT[1]), f32), pltpu.VMEM((64, WIDE), f32)),
             dma((CHUNKS,)), dma, dma((2,)), dma((8,)), dma,
-            dma((CHUNKS,)), dma((CHUNKS,)), dma, dma,
+            dma((CHUNKS,)), dma((CHUNKS,)), dma((6,)), dma((6,)),
             dma((14,)), dma((8, 2)), dma((8, 2)), dma((8, 2)),
         ],
         compiler_params=pltpu.CompilerParams(
@@ -402,7 +430,7 @@
     act_grad, partial = call(
         cotangent, jnp.swapaxes(pre_act, 0, 1), jnp.swapaxes(down_weight, 0, 1), tile_expert, tile_fill
     )
-    return jnp.swapaxes(act_grad, 0, 1), jnp.swapaxes(partial.reshape(2, 8, WIDTH), 0, 1)
+    return act_grad, jnp.swapaxes(partial.reshape(2, 8, WIDTH), 0, 1)
 
 
 def solution(mesh):

time: 108 us -> 119 us (1.10)
  the two profiles are of different devices: /device:TPU:0 before, /device:TPU:1 now
where the time goes in v3:
time: 119 us; the launch traced here: 118 us
  Pallas kernels  104 us (87%)
  local copies, waits for them, and re-layouts  14.2 us (12%)
    pallas_call x1, Pallas kernels, call(): pl.pallas_call(kernel, out_shape=(jax.ShapeDtypeStruct((ROWS, 2, HIDDEN),...  104 us
    unnamed x3, local copies, waits for them, and re-layouts  12.4 us

profile of v3, /device:TPU:1, one launch (start us, length us, event | category | flops | bytes accessed | tf_op | source)
XLA Modules:
  0.0 118.4 jit_solution(3573272550495925739)
XLA Ops:
  0.6 2.2 %copy.14 = bf16[64,2,3584]{2,0,1:T(8,128)(2,1)} copy(bf16[64,2,3584]{2,1,0:T(2,128)(2,1)} %param.7) | data formatting | bytes 1835008 | tf_op args[2]
  2.8 4.5 %copy.13 = bf16[768,2,1024]{2,0,1:T(8,128)(2,1)} copy(bf16[768,2,1024]{2,1,0:T(2,128)(2,1)} %param.6) | data formatting | bytes 6291456 | tf_op args[1]
  7.4 103.5 %shard_map.68 = (bf16[768,2,1024]{2,1,0:T(2,128)(2,1)}, f32[16,3584]{1,0:T(8,128)}) custom-call(bf16[768,3584]{1,0:T(8,128)(2,1)} %cot_hbm.1, bf16[2,768,1024]{2,1,0:T(8,128)(2,1)} %bitcast.10, bf16[2,64,3584]{2,1,0:T(8,128)(2,1)} %bitcast.11, s32[6]{0:T(128)} %expert_ref.1, s32[6]{0:T(128)} %fill_ref.1), custom_call_target="tpu_custom_call" | custom-call | flops 24000000000 | bytes 30000000 | tf_op jit(solution)/shard_map/pallas_call | solution.py:393
  110.9 1.8 %copy.15 = f32[2,8,3584]{2,0,1:T(2,128)} copy(f32[2,8,3584]{2,1,0:T(8,128)} %bitcast.13) | data formatting | bytes 458752 | tf_op jit(solution)/shard_map/reshape | solution.py:433
  112.7 5.7 %copy.17 = bf16[768,2,1024]{2,1,0:T(2,128)(2,1)} copy(bf16[768,2,1024]{2,1,0:T(2,128)(2,1)} %get-tuple-element.8) | data formatting | bytes 6291456

commit v4 on v3

--- a/solution.py
+++ b/solution.py
@@ -19,8 +19,9 @@
 f32 = jnp.float32
 bf16 = jnp.bfloat16
 
-EVENTS = {1: ((1, 0), (2, 1)), 2: ((1, 1), (2, 0), (4, 0), (4, 1)), 4: ((3, 0), (3, 1)),
-          5: ((5, 0), (6, 1)), 7: ((5, 1), (6, 0)), 10: ((7, 0), (7, 1))}
+EVENTS = {1: ((1, 0), (2, 1), (4, 0)), 3: ((1, 1), (2, 0)), 4: ((4, 1), (3, 0), (3, 1)),
+          6: ((5, 0), (6, 0)), 7: ((5, 1), (6, 1)), 10: ((7, 0), (7, 1))}
+HOPS = (1, 2)
 ORDER = (0, 1, 2, 4, 3, 5, 6, 7)
 TURNS = {2: (0,), 3: (1,), 4: (2,), 5: (3,), 6: (4,), 8: (5,), 9: (6,), 10: (7,)}
 
@@ -32,7 +33,7 @@
     rings, directs, tot,
     cot_sem, pre_sem, w_sem, grad_sem, out_sem,
     cs_send, cs_recv, ls_send, ls_recv,
-    ag_send, ag_recv, sib_send, sib_recv,
+    ag_send, ag_recv, sib_send, sib_recv, hop_send, hop_recv,
 ):
     g = lax.axis_index("group")
     b = lax.axis_index("blk")
@@ -106,9 +107,21 @@
         block = w_all.at[piece(src_j), e, c]
         return remote(block, block, ag_send.at[slot], ag_recv.at[dst_j, e], device_id)
 
+    def hop(i):
+        block = w_all.at[piece(0), 1, c, pl.ds(i * 32, 32)]
+        return remote(block, block, hop_send.at[i], hop_recv.at[i], x_peer)
+
+    def hop_wait(i):
+        block = w_all.at[piece(4), 1, c, pl.ds(i * 32, 32)]
+        remote(block, block, hop_send.at[i], hop_recv.at[i], x_peer).wait_recv()
+
     def gather_wait(j, e):
-        block = w_all.at[piece(j), e, c]
-        remote(block, block, ag_send.at[0], ag_recv.at[j, e], sibling).wait_recv()
+        if (j, e) == (4, 1):
+            for i in range(2):
+                hop_wait(i)
+        else:
+            block = w_all.at[piece(j), e, c]
+            remote(block, block, ag_send.at[0], ag_recv.at[j, e], sibling).wait_recv()
 
     def share(j, e):
         block = w_all.at[piece(j), e, c]
@@ -118,7 +131,7 @@
         block = w_all.at[piece(j), e, other]
         remote(block, block, sib_send.at[j, e], sib_recv.at[j, e], sibling).wait_recv()
 
-    sends = [(0, 1, 0, y_up), (0, 2, 1, y_dn), (0, 4, 0, x_peer), (0, 4, 1, x_peer), (0, 1, 1, y_up), (0, 2, 0, y_dn)]
+    sends = [(0, 1, 0, y_up), (0, 2, 1, y_dn), (0, 4, 0, x_peer), (0, 1, 1, y_up), (0, 2, 0, y_dn)]
     sends += [(1, 3, 0, y_up), (2, 3, 1, y_dn)]
     for e in range(2):
         sends += [(4, 5, e, y_up), (4, 6, e, y_dn)]
@@ -137,7 +150,7 @@
     cot_remote(0).start()
     for e in range(2):
         w_copy(e).wait()
-    for slot in range(6):
+    for slot in range(5):
         gather(slot).start()
 
     pre_copy().wait()
@@ -235,13 +248,13 @@
         for i, offset in ((2, 2), (0, 1), (1, 3)):
             out[k, i] = load(lax.rem(direct_of[st][0] + offset, 4)).astype(out.dtype)
             direct_copy(st, k, i).start()
-        own[lax.rem(k, 2)] = load(direct_of[st][0])
+        own[k] = load(direct_of[st][0])
 
     def collected(st, k):
         _, came, own, _, _ = directs[st]
         for i in range(3):
             direct_copy(st, k, i).wait_recv()
-        return own[lax.rem(k, 2)] + came[k, 0].astype(f32) + came[k, 1].astype(f32) + came[k, 2].astype(f32)
+        return own[k] + came[k, 0].astype(f32) + came[k, 1].astype(f32) + came[k, 2].astype(f32)
 
     def make(k):
         cot_remote(k).wait_recv()
@@ -267,7 +280,9 @@
         spread(2, k, lambda at: tot[2][pl.ds(pl.multiple_of(at * 16, 16), 16), :])
 
     def last(k):
-        out_buf[:, cot_cols(k)] = collected(2, k) * grad_factor
+        value = collected(2, k) * grad_factor
+        for e in range(2):
+            out_buf[:, e, cot_cols(k)] = value[e * 8:e * 8 + 8]
 
     def grad_copy(turn):
         cols = pl.ds(pl.multiple_of(piece(ORDER[turn]) * 128, 128), 128)
@@ -323,18 +338,23 @@
             def _():
                 do()
 
+        for i in range(2):
+            on(HOPS[i], lambda: hop(i).start())
         for when, those in EVENTS.items():
             for j, e in those:
                 on(when, functools.partial(arrived, j, e))
         at(0, make)
         at(1, relay)
         at(2, onward)
-        at(3, joined)
-        at(4, last)
+        at(4, joined)
 
         for when, those in TURNS.items():
             for turn in those:
                 on(when, functools.partial(hidden, turn))
+
+    @pl.loop(0, CHUNKS)
+    def _(k):
+        last(k)
 
     out = pltpu.make_async_copy(out_buf, wgrad_hbm, out_sem)
     out.start()
@@ -359,6 +379,8 @@
 
     for slot in range(len(sends)):
         gather(slot).wait_send()
+    for i in range(2):
+        hop(i).wait_send()
     for j in range(8):
         for e in range(2):
             share(j, e).wait_send()
@@ -380,7 +402,7 @@
     return (
         pltpu.VMEM((CHUNKS, 3, rows, cols), kind),
         pltpu.VMEM((CHUNKS, 3, rows, cols), kind),
-        pltpu.VMEM((2, rows, cols), f32),
+        pltpu.VMEM((CHUNKS, rows, cols), f32),
         dma((CHUNKS, 3)),
         dma((CHUNKS, 3)),
     )
@@ -394,7 +416,7 @@
         kernel,
         out_shape=(
             jax.ShapeDtypeStruct((ROWS, 2, HIDDEN), bf16),
-            jax.ShapeDtypeStruct((16, WIDTH), f32),
+            jax.ShapeDtypeStruct((8, 2, WIDTH), f32),
         ),
         in_specs=[any_space, any_space, any_space, scalars, scalars],
         out_specs=(any_space, any_space),
@@ -406,7 +428,7 @@
             pltpu.VMEM((4, 4, 64, ROWS), bf16),
             pltpu.VMEM((8, 2, 2, 64, WIDTH), bf16),
             pltpu.VMEM((2, ROWS, 2, 128), bf16),
-            pltpu.VMEM((16, WIDTH), f32),
+            pltpu.VMEM((8, 2, WIDTH), f32),
             pltpu.VMEM((4, 4, 64, SPLIT[1]), f32),
             tuple(ring_scratch(256, cols, bf16) for cols in SPLIT),
             (
@@ -417,7 +439,7 @@
             (pltpu.VMEM((256, SPLIT[0]), f32), pltpu.VMEM((256, SPLIT[1]), f32), pltpu.VMEM((64, WIDE), f32)),
             dma((CHUNKS,)), dma, dma((2,)), dma((8,)), dma,
             dma((CHUNKS,)), dma((CHUNKS,)), dma((6,)), dma((6,)),
-            dma((14,)), dma((8, 2)), dma((8, 2)), dma((8, 2)),
+            dma((13,)), dma((8, 2)), dma((8, 2)), dma((8, 2)), dma((2,)), dma((2,)),
         ],
         compiler_params=pltpu.CompilerParams(
             collective_id=0, has_side_effects=True, vmem_limit_bytes=60 * 2**20
@@ -426,11 +448,39 @@
     )(cot, pre, w, expert, fill)
 
 
+def hand_on(act_in, wgrad_in, act_out, wgrad_out, act_buf, wgrad_buf, in_sems, out_sems):
+    parts = 8
+    rows = ROWS // parts
+    slices = [pl.ds(i * rows, rows) for i in range(parts)]
+    ins = [pltpu.make_async_copy(act_in.at[r], act_buf.at[r], in_sems.at[i]) for i, r in enumerate(slices)]
+    outs = [pltpu.make_async_copy(act_buf.at[r], act_out.at[r], out_sems.at[i]) for i, r in enumerate(slices)]
+    ins.append(pltpu.make_async_copy(wgrad_in, wgrad_buf, in_sems.at[parts]))
+    outs.append(pltpu.make_async_copy(wgrad_buf, wgrad_out, out_sems.at[parts]))
+    for copy in ins:
+        copy.start()
+    for came, copy in zip(ins, outs):
+        came.wait()
+        copy.start()
+    for copy in outs:
+        copy.wait()
+
+
 def body(cotangent, pre_act, down_weight, tile_expert, tile_fill):
-    act_grad, partial = call(
+    results = call(
         cotangent, jnp.swapaxes(pre_act, 0, 1), jnp.swapaxes(down_weight, 0, 1), tile_expert, tile_fill
     )
-    return act_grad, jnp.swapaxes(partial.reshape(2, 8, WIDTH), 0, 1)
+    any_space = pl.BlockSpec(memory_space=pl.ANY)
+    return pl.pallas_call(
+        hand_on,
+        out_shape=tuple(jax.ShapeDtypeStruct(r.shape, r.dtype) for r in results),
+        in_specs=[any_space] * 2,
+        out_specs=(any_space,) * 2,
+        scratch_shapes=[
+            pltpu.VMEM((ROWS, 2, HIDDEN), bf16), pltpu.VMEM((8, 2, WIDTH), f32),
+            pltpu.SemaphoreType.DMA((9,)), pltpu.SemaphoreType.DMA((9,)),
+        ],
+        compiler_params=pltpu.CompilerParams(vmem_limit_bytes=16 * 2**20),
+    )(*results)
 
 
 def solution(mesh):

time: 119 us -> 99.5 us (0.84)
  Pallas kernels: 104 us -> 89 us
  local copies, waits for them, and re-layouts: 14.2 us -> 9.54 us
    pallas_call x1, Pallas kernels: 104 us -> 85.4 us  [call(): pl.pallas_call(kernel, out_shape=(jax.ShapeDtypeStruct((ROWS, 2, HIDDEN),...]
    pallas_call x0 -> x1, Pallas kernels: none -> 3.66 us  [body(): pl.pallas_call(hand_on, out_shape=tuple((jax.ShapeDtypeStruct(r.shape, r....]
    unnamed x3 -> x6, local copies, waits for them, and re-layouts: 12.4 us -> 9.54 us
    reshape x1 -> x0, local copies, waits for them, and re-layouts: 1.8 us -> none  [body(): return (act_grad, jnp.swapaxes(partial.reshape(2, 8, WIDTH), 0, 1))]
where the time goes in v4:
time: 99.5 us; the launch traced here: 99.2 us
  Pallas kernels  89 us (89%)
  local copies, waits for them, and re-layouts  9.54 us (10%)
    pallas_call x1, Pallas kernels, call(): pl.pallas_call(kernel, out_shape=(jax.ShapeDtypeStruct((ROWS, 2, HIDDEN),...  85.4 us
    unnamed x6, local copies, waits for them, and re-layouts  9.54 us
    pallas_call x1, Pallas kernels, body(): pl.pallas_call(hand_on, out_shape=tuple((jax.ShapeDtypeStruct(r.shape, r....  3.66 us

profile of v4, /device:TPU:1, one launch (start us, length us, event | category | flops | bytes accessed | tf_op | source)
XLA Modules:
  0.0 99.2 jit_solution(4689367072676199379)
XLA Ops:
  0.6 2.2 %copy.12 = bf16[64,2,3584]{2,0,1:T(8,128)(2,1)} copy(bf16[64,2,3584]{2,1,0:T(2,128)(2,1)} %param.7) | data formatting | bytes 1835008 | tf_op args[2]
  2.8 4.5 %copy.11 = bf16[768,2,1024]{2,0,1:T(8,128)(2,1)} copy(bf16[768,2,1024]{2,1,0:T(2,128)(2,1)} %param.6) | data formatting | bytes 6291456 | tf_op args[1]
  7.3 85.4 %shard_map.68 = (bf16[768,2,1024]{2,1,0:T(2,128)(2,1)}, f32[8,2,3584]{2,1,0:T(2,128)}) custom-call(bf16[768,3584]{1,0:T(8,128)(2,1)} %cot_hbm.1, bf16[2,768,1024]{2,1,0:T(8,128)(2,1)} %bitcast.6, bf16[2,64,3584]{2,1,0:T(8,128)(2,1)} %bitcast.7, s32[6]{0:T(128)} %expert_ref.1, s32[6]{0:T(128)} %fill_ref.1), custom_call_target="tpu_custom_call" | custom-call | flops 24000000000 | bytes 30000000 | tf_op jit(solution)/shard_map/pallas_call | solution.py:415
  92.7 0.0 copy-start
  92.8 1.9 %copy-done = bf16[768,2,1024]{2,1,0:T(2,128)(2,1)S(1)} copy-done((bf16[768,2,1024]{2,1,0:T(2,128)(2,1)S(1)}, bf16[768,2,1024]{2,1,0:T(2,128)(2,1)}, u32[]{:S(2)}) %copy-start) | copy-done | bytes 3145752
  94.6 0.0 copy-start.1
  94.6 0.9 copy-done.1
  95.6 3.7 %shard_map.69 = (bf16[768,2,1024]{2,1,0:T(2,128)(2,1)}, f32[8,2,3584]{2,1,0:T(2,128)}) custom-call(bf16[768,2,1024]{2,1,0:T(2,128)(2,1)S(1)} %copy-done, f32[8,2,3584]{2,1,0:T(2,128)S(1)} %copy-done.1), custom_call_target="tpu_custom_call" | custom-call | tf_op jit(solution)/shard_map/pallas_call | solution.py:473
Async XLA Ops:
  92.7 1.9 %copy-start = (bf16[768,2,1024]{2,1,0:T(2,128)(2,1)S(1)}, bf16[768,2,1024]{2,1,0:T(2,128)(2,1)}, u32[]{:S(2)}) copy-start(bf16[768,2,1024]{2,1,0:T(2,128)(2,1)} %get-tuple-element.4.act_in) | copy-start | bytes 9437188
  94.6 0.9 copy-start.1

commit v5 on v4

--- a/solution.py
+++ b/solution.py
@@ -29,7 +29,7 @@
 def kernel(
     cot_hbm, pre_hbm, w_hbm, expert_ref, fill_ref,
     act_hbm, wgrad_hbm,
-    cot_own, cot_sib, pre, lhs, lhs_sib, w_all, grad_buf, out_buf, mixed,
+    cot_own, cot_sib, raw, pre, lhs, lhs_sib, w_all, grad_buf, out_buf, mixed,
     rings, directs, tot,
     cot_sem, pre_sem, w_sem, grad_sem, out_sem,
     cs_send, cs_recv, ls_send, ls_recv,
@@ -64,8 +64,9 @@
     def cot_copy(k):
         return pltpu.make_async_copy(cot_hbm.at[:, cot_cols(k)], cot_own.at[:, cot_cols(k)], cot_sem.at[k])
 
-    def pre_copy():
-        return pltpu.make_async_copy(pre_hbm, pre, pre_sem)
+    def pre_copy(part):
+        cols = pl.ds(pl.multiple_of(part * 128, 128), 128)
+        return pltpu.make_async_copy(pre_hbm.at[:, :, cols], raw.at[part], pre_sem.at[part])
 
     q_own = y * 2 + x_hi
 
@@ -74,7 +75,10 @@
 
     for e in range(2):
         w_copy(e).start()
-    pre_copy().start()
+
+    @pl.loop(0, 8)
+    def _(part):
+        pre_copy(part).start()
 
     @pl.loop(0, CHUNKS)
     def _(k):
@@ -153,7 +157,15 @@
     for slot in range(5):
         gather(slot).start()
 
-    pre_copy().wait()
+    for part in range(8):
+        pre_copy(part).wait()
+
+        @pl.loop(0, ROWS // 128)
+        def _(t):
+            rows = pl.ds(pl.multiple_of(t * 128, 128), 128)
+            both = raw[part, rows].astype(f32)
+            for i in range(2):
+                pre[i, rows, part * 128:part * 128 + 128] = both[:, i, :].astype(bf16)
 
     @pl.loop(0, ROWS // 128)
     def _(t):
@@ -168,7 +180,7 @@
             cols = pl.ds(pl.multiple_of(part * 128, 128), 128)
             gate = pre[0, rows, cols].astype(f32)
             up = pre[1, rows, cols].astype(f32)
-            sig = 1.0 / (1.0 + jnp.exp(-gate))
+            sig = jax.nn.sigmoid(gate)
             turned = jnp.transpose(gate * sig * up)
             part_x, part_z = lax.div(part, 4), lax.rem(part, 4)
             for yy in range(4):
@@ -312,7 +324,7 @@
                 grad = jnp.where(alive, jnp.where(second, both[:, 128:], both[:, :128]), 0.0)
                 gate = pre[0, part, cols].astype(f32)
                 up = pre[1, part, cols].astype(f32)
-                sig = 1.0 / (1.0 + jnp.exp(-gate))
+                sig = jax.nn.sigmoid(gate)
                 grad_buf[turn % 2, part, 0, :] = (grad * up * sig * (1.0 + gate * (1.0 - sig))).astype(bf16)
                 grad_buf[turn % 2, part, 1, :] = (grad * (gate * sig)).astype(bf16)
 
@@ -418,11 +430,12 @@
             jax.ShapeDtypeStruct((ROWS, 2, HIDDEN), bf16),
             jax.ShapeDtypeStruct((8, 2, WIDTH), f32),
         ),
-        in_specs=[any_space, any_space, any_space, scalars, scalars],
+        in_specs=[any_space, pl.BlockSpec(memory_space=pltpu.HBM), any_space, scalars, scalars],
         out_specs=(any_space, any_space),
         scratch_shapes=[
             pltpu.VMEM((ROWS, WIDTH), bf16),
             pltpu.VMEM((ROWS, WIDTH), bf16),
+            pltpu.VMEM((8, ROWS, 2, 128), bf16),
             pltpu.VMEM((2, ROWS, HIDDEN), bf16),
             pltpu.VMEM((2, 4, 4, 64, ROWS), bf16),
             pltpu.VMEM((4, 4, 64, ROWS), bf16),
@@ -437,7 +450,7 @@
                 direct_scratch(16, WIDE, f32),
             ),
             (pltpu.VMEM((256, SPLIT[0]), f32), pltpu.VMEM((256, SPLIT[1]), f32), pltpu.VMEM((64, WIDE), f32)),
-            dma((CHUNKS,)), dma, dma((2,)), dma((8,)), dma,
+            dma((CHUNKS,)), dma((8,)), dma((2,)), dma((8,)), dma,
             dma((CHUNKS,)), dma((CHUNKS,)), dma((6,)), dma((6,)),
             dma((13,)), dma((8, 2)), dma((8, 2)), dma((8, 2)), dma((2,)), dma((2,)),
         ],
@@ -449,7 +462,7 @@
 
 
 def hand_on(act_in, wgrad_in, act_out, wgrad_out, act_buf, wgrad_buf, in_sems, out_sems):
-    parts = 8
+    parts = 4
     rows = ROWS // parts
     slices = [pl.ds(i * rows, rows) for i in range(parts)]
     ins = [pltpu.make_async_copy(act_in.at[r], act_buf.at[r], in_sems.at[i]) for i, r in enumerate(slices)]
@@ -467,19 +480,19 @@
 
 def body(cotangent, pre_act, down_weight, tile_expert, tile_fill):
     results = call(
-        cotangent, jnp.swapaxes(pre_act, 0, 1), jnp.swapaxes(down_weight, 0, 1), tile_expert, tile_fill
+        cotangent, pre_act, jnp.swapaxes(down_weight, 0, 1), tile_expert, tile_fill
     )
     any_space = pl.BlockSpec(memory_space=pl.ANY)
     return pl.pallas_call(
         hand_on,
         out_shape=tuple(jax.ShapeDtypeStruct(r.shape, r.dtype) for r in results),
-        in_specs=[any_space] * 2,
+        in_specs=[pl.BlockSpec(memory_space=pltpu.HBM)] * 2,
         out_specs=(any_space,) * 2,
         scratch_shapes=[
             pltpu.VMEM((ROWS, 2, HIDDEN), bf16), pltpu.VMEM((8, 2, WIDTH), f32),
             pltpu.SemaphoreType.DMA((9,)), pltpu.SemaphoreType.DMA((9,)),
         ],
-        compiler_params=pltpu.CompilerParams(vmem_limit_bytes=16 * 2**20),
+        compiler_params=pltpu.CompilerParams(vmem_limit_bytes=60 * 2**20),
     )(*results)
 
 

time: 99.5 us -> 95.1 us (0.956)
  the two profiles are of different devices: /device:TPU:1 before, /device:TPU:0 now
where the time goes in v5:
time: 95.1 us; the launch traced here: 93.6 us
  Pallas kernels  90.7 us (95%)
  local copies, waits for them, and re-layouts  2.19 us (2%)
    pallas_call x1, Pallas kernels, call(): pl.pallas_call(kernel, out_shape=(jax.ShapeDtypeStruct((ROWS, 2, HIDDEN),...  87.7 us
    pallas_call x1, Pallas kernels, body(): pl.pallas_call(hand_on, out_shape=tuple((jax.ShapeDtypeStruct(r.shape, r....  3.01 us
    unnamed x1, local copies, waits for them, and re-layouts  2.19 us

profile of v5, /device:TPU:0, one launch (start us, length us, event | category | flops | bytes accessed | tf_op | source)
XLA Modules:
  0.0 93.6 jit_solution(9734708526230046575)
XLA Ops:
  0.6 2.2 %copy.9 = bf16[64,2,3584]{2,0,1:T(8,128)(2,1)} copy(bf16[64,2,3584]{2,1,0:T(2,128)(2,1)} %param.7) | data formatting | bytes 1835008 | tf_op args[2]
  2.8 87.7 %shard_map.68 = (bf16[768,2,1024]{2,1,0:T(2,128)(2,1)}, f32[8,2,3584]{2,1,0:T(2,128)}) custom-call(bf16[768,3584]{1,0:T(8,128)(2,1)} %cot_hbm.1, bf16[768,2,1024]{2,1,0:T(2,128)(2,1)} %pre_hbm.1, bf16[2,64,3584]{2,1,0:T(8,128)(2,1)} %bitcast.3, s32[6]{0:T(128)} %expert_ref.1, s32[6]{0:T(128)} %fill_ref.1), custom_call_target="tpu_custom_call" | custom-call | flops 24000000000 | bytes 30000000 | tf_op jit(solution)/shard_map/pallas_call | solution.py:427
  90.5 3.0 %shard_map.69 = (bf16[768,2,1024]{2,1,0:T(2,128)(2,1)}, f32[8,2,3584]{2,1,0:T(2,128)}) custom-call(bf16[768,2,1024]{2,1,0:T(2,128)(2,1)} %get-tuple-element.4.act_in, f32[8,2,3584]{2,1,0:T(2,128)} %get-tuple-element.5.wgrad_in), custom_call_target="tpu_custom_call" | custom-call | tf_op jit(solution)/shard_map/pallas_call | solution.py:486

commit v6 on v5

--- a/solution.py
+++ b/solution.py
@@ -15,15 +15,15 @@
 WIDTH = 3584
 WIDE = 512
 CHUNKS = WIDTH // WIDE
-SPLIT = (384, 128)
+SPLIT = (256, 256)
 f32 = jnp.float32
 bf16 = jnp.bfloat16
 
-EVENTS = {1: ((1, 0), (2, 1), (4, 0)), 3: ((1, 1), (2, 0)), 4: ((4, 1), (3, 0), (3, 1)),
-          6: ((5, 0), (6, 0)), 7: ((5, 1), (6, 1)), 10: ((7, 0), (7, 1))}
-HOPS = (1, 2)
+EVENTS = {0: ((1, 0), (2, 1)), 1: ((4, 0),), 2: ((1, 1),), 3: ((2, 0),), 4: ((3, 0), (4, 1)), 5: ((5, 0),),
+          6: ((3, 1), (6, 1)), 7: ((5, 1),), 8: ((6, 0),), 9: ((7, 0), (7, 1))}
+HOPS = (0, 3)
 ORDER = (0, 1, 2, 4, 3, 5, 6, 7)
-TURNS = {2: (0,), 3: (1,), 4: (2,), 5: (3,), 6: (4,), 8: (5,), 9: (6,), 10: (7,)}
+TURNS = {2: (0,), 3: (1, 2), 5: (3,), 6: (4,), 7: (5,), 9: (6,), 10: (7,)}
 
 
 def kernel(
@@ -462,7 +462,7 @@
 
 
 def hand_on(act_in, wgrad_in, act_out, wgrad_out, act_buf, wgrad_buf, in_sems, out_sems):
-    parts = 4
+    parts = 8
     rows = ROWS // parts
     slices = [pl.ds(i * rows, rows) for i in range(parts)]
     ins = [pltpu.make_async_copy(act_in.at[r], act_buf.at[r], in_sems.at[i]) for i, r in enumerate(slices)]

time: 95.1 us -> 91.1 us (0.958); the launches traced: 93.6 us -> 91 us
  Pallas kernels: 90.7 us -> 88.1 us
    pallas_call x1, Pallas kernels: 87.7 us -> 85.2 us  [call(): pl.pallas_call(kernel, out_shape=(jax.ShapeDtypeStruct((ROWS, 2, HIDDEN),...]
where the time goes in v6:
time: 91.1 us; the launch traced here: 91 us
  Pallas kernels  88.1 us (97%)
  local copies, waits for them, and re-layouts  2.19 us (2%)
    pallas_call x1, Pallas kernels, call(): pl.pallas_call(kernel, out_shape=(jax.ShapeDtypeStruct((ROWS, 2, HIDDEN),...  85.2 us
    pallas_call x1, Pallas kernels, body(): pl.pallas_call(hand_on, out_shape=tuple((jax.ShapeDtypeStruct(r.shape, r....  2.88 us
    unnamed x1, local copies, waits for them, and re-layouts  2.19 us

profile of v6, /device:TPU:0, one launch (start us, length us, event | category | flops | bytes accessed | tf_op | source)
XLA Modules:
  0.0 91.0 jit_solution(15246021058178603265)
XLA Ops:
  0.6 2.2 %copy.9 = bf16[64,2,3584]{2,0,1:T(8,128)(2,1)} copy(bf16[64,2,3584]{2,1,0:T(2,128)(2,1)} %param.7) | data formatting | bytes 1835008 | tf_op args[2]
  2.8 85.2 %shard_map.68 = (bf16[768,2,1024]{2,1,0:T(2,128)(2,1)}, f32[8,2,3584]{2,1,0:T(2,128)}) custom-call(bf16[768,3584]{1,0:T(8,128)(2,1)} %cot_hbm.1, bf16[768,2,1024]{2,1,0:T(2,128)(2,1)} %pre_hbm.1, bf16[2,64,3584]{2,1,0:T(8,128)(2,1)} %bitcast.3, s32[6]{0:T(128)} %expert_ref.1, s32[6]{0:T(128)} %fill_ref.1), custom_call_target="tpu_custom_call" | custom-call | flops 24000000000 | bytes 30000000 | tf_op jit(solution)/shard_map/pallas_call | solution.py:427
  88.1 2.9 %shard_map.69 = (bf16[768,2,1024]{2,1,0:T(2,128)(2,1)}, f32[8,2,3584]{2,1,0:T(2,128)}) custom-call(bf16[768,2,1024]{2,1,0:T(2,128)(2,1)} %get-tuple-element.4.act_in, f32[8,2,3584]{2,1,0:T(2,128)} %get-tuple-element.5.wgrad_in), custom_call_target="tpu_custom_call" | custom-call | tf_op jit(solution)/shard_map/pallas_call | solution.py:486

commit v7 on v6

--- a/solution.py
+++ b/solution.py
@@ -23,7 +23,7 @@
           6: ((3, 1), (6, 1)), 7: ((5, 1),), 8: ((6, 0),), 9: ((7, 0), (7, 1))}
 HOPS = (0, 3)
 ORDER = (0, 1, 2, 4, 3, 5, 6, 7)
-TURNS = {2: (0,), 3: (1, 2), 5: (3,), 6: (4,), 7: (5,), 9: (6,), 10: (7,)}
+TURNS = {2: (0, 1), 3: (2,), 5: (3,), 6: (4,), 7: (5,), 9: (6,), 10: (7,)}
 
 
 def kernel(

time: 91.1 us -> 92.9 us (1.020); the launches traced: 91 us -> 91.7 us
  no operation moved by 1% of the time
where the time goes in v7:
time: 92.9 us; the launch traced here: 91.7 us
  Pallas kernels  88.9 us (96%)
  local copies, waits for them, and re-layouts  2.19 us (2%)
    pallas_call x1, Pallas kernels, call(): pl.pallas_call(kernel, out_shape=(jax.ShapeDtypeStruct((ROWS, 2, HIDDEN),...  86 us
    pallas_call x1, Pallas kernels, body(): pl.pallas_call(hand_on, out_shape=tuple((jax.ShapeDtypeStruct(r.shape, r....  2.88 us
    unnamed x1, local copies, waits for them, and re-layouts  2.19 us

profile of v7, /device:TPU:0, one launch (start us, length us, event | category | flops | bytes accessed | tf_op | source)
XLA Modules:
  0.0 91.7 jit_solution(8199454950725748918)
XLA Ops:
  0.6 2.2 %copy.9 = bf16[64,2,3584]{2,0,1:T(8,128)(2,1)} copy(bf16[64,2,3584]{2,1,0:T(2,128)(2,1)} %param.7) | data formatting | bytes 1835008 | tf_op args[2]
  2.8 86.0 %shard_map.68 = (bf16[768,2,1024]{2,1,0:T(2,128)(2,1)}, f32[8,2,3584]{2,1,0:T(2,128)}) custom-call(bf16[768,3584]{1,0:T(8,128)(2,1)} %cot_hbm.1, bf16[768,2,1024]{2,1,0:T(2,128)(2,1)} %pre_hbm.1, bf16[2,64,3584]{2,1,0:T(8,128)(2,1)} %bitcast.3, s32[6]{0:T(128)} %expert_ref.1, s32[6]{0:T(128)} %fill_ref.1), custom_call_target="tpu_custom_call" | custom-call | flops 24000000000 | bytes 30000000 | tf_op jit(solution)/shard_map/pallas_call | solution.py:427
  88.8 2.9 %shard_map.69 = (bf16[768,2,1024]{2,1,0:T(2,128)(2,1)}, f32[8,2,3584]{2,1,0:T(2,128)}) custom-call(bf16[768,2,1024]{2,1,0:T(2,128)(2,1)} %get-tuple-element.4.act_in, f32[8,2,3584]{2,1,0:T(2,128)} %get-tuple-element.5.wgrad_in), custom_call_target="tpu_custom_call" | custom-call | tf_op jit(solution)/shard_map/pallas_call | solution.py:486
